TPU v7x, 128 devices: a whole 4x4x4 slice. The times are simulated.
128 devices in a mesh: gx: 8 (over z, x_lo), gy: 4 (over x_hi, core), ha: 4 (over y).
Axes of the slice: x: 4 (x_hi: 2, x_lo: 2; x = x_hi * 2 + x_lo), y: 4, z: 4, core: 2. Of those that a mesh axis runs over, the one named last changes fastest.
Arguments:
- tokens: bfloat16 [64, 64, 16, 384], P('gx', 'gy'), may hold values from -30 to 30
- input_weight: bfloat16 [384, 768], P(None, 'ha'), may hold values from -1 to 1
- output_weight: bfloat16 [256, 384], P('ha'), may hold values from -0.375 to 0.375
- tissue_bits: int32 [64, 64], P('gx', 'gy'), may hold values from 0 to 65535
- cotangent: bfloat16 [64, 64, 16, 384], P('gx', 'gy'), may hold values from -6 to 6
Outputs:
- token_gradient: bfloat16 [64, 64, 16, 384], P('gx', 'gy', None, 'ha')
- input_gradient: float32 [384, 768], P(None, 'ha')
- output_gradient: float32 [256, 384], P('ha')
All inputs are finite; a program needn't handle non-finite values.
Results may differ from a plain program's by a relative error of at most 0.018.
The roundings to bfloat16 on the way count: a program that leaves them out, or rounds other values in their place, can miss the bound.
Values may be sent and summed in bfloat16 or wider, within the bound.
No kernel may reach another device: no remote copies, remote signals or barrier semaphores. Data moves between devices by JAX's collectives and lax.ppermute only.
A program may use at most 128 MiB of HBM per device.

v0:
```python
import jax
import jax.numpy as jnp
from jax import lax
from jax.sharding import PartitionSpec as P

HD = 64
REACH = 3


def extended(block, sides, width):
    for axis, dim in sides:
        count = lax.axis_size(axis)
        forward = [(i, i + 1) for i in range(count - 1)]
        backward = [(target, source) for source, target in forward]
        low = lax.ppermute(
            lax.slice_in_dim(block, block.shape[dim] - width, None, axis=dim), axis, forward
        )
        high = lax.ppermute(lax.slice_in_dim(block, 0, width, axis=dim), axis, backward)
        block = jnp.concatenate([low, block, high], axis=dim)
    return block


def block_length(extent, plane_rows):
    for length in range(1, extent + 1):
        if extent % length == 0 and length * plane_rows >= 512:
            return length
    return extent


def shards(tokens, input_weight, output_weight, tissue_bits, cotangent):
    width_x, width_y, depth, model_width = tokens.shape
    local_heads = output_weight.shape[0] // HD
    token_count = width_x * width_y * depth
    score_scale = HD ** (-0.5)
    flat_tokens = tokens.reshape(token_count, model_width)
    flat_cotangent = cotangent.reshape(token_count, model_width)
    bit_values = 2 ** jnp.arange(depth, dtype=jnp.int32)
    key_valid = (tissue_bits[:, :, None] // bit_values % 2).astype(jnp.bfloat16)
    key_span_x_full = width_x + 2 * REACH
    key_span_y = width_y + 2 * REACH
    projected = jnp.dot(flat_tokens, input_weight, preferred_element_type=jnp.float32).astype(
        jnp.bfloat16
    )
    projected = projected.reshape(token_count, local_heads, 3, HD)
    queries = projected[:, :, 0, :].reshape(token_count, local_heads * HD)
    pair_local = projected[:, :, 1:, :].reshape(width_x, width_y, depth, local_heads * 2 * HD)
    pair_padded, valid_padded = (
        extended(pair_local, (("gx", 0), ("gy", 1)), REACH),
        extended(key_valid, (("gx", 0), ("gy", 1)), REACH),
    )
    upstream = jnp.einsum(
        "nd,ed->ne", flat_cotangent, output_weight, preferred_element_type=jnp.float32
    ).astype(jnp.bfloat16)
    block_x = block_length(width_x, width_y * depth)
    block_count = width_x // block_x
    key_span_x = block_x + 2 * REACH
    query_rows = block_x * width_y * depth
    key_rows = key_span_x * key_span_y * depth
    query_slots = jnp.arange(query_rows)
    query_x = query_slots // (width_y * depth)
    query_y = query_slots // depth % width_y
    query_z = query_slots % depth
    key_slots = jnp.arange(key_rows)
    key_x = key_slots // (key_span_y * depth) - REACH
    key_y = key_slots // depth % key_span_y - REACH
    key_z = key_slots % depth
    within = (
        (jnp.abs(query_x[:, None] - key_x[None, :]) <= REACH)
        & (jnp.abs(query_y[:, None] - key_y[None, :]) <= REACH)
        & (jnp.abs(query_z[:, None] - key_z[None, :]) <= REACH)
    )
    self_pair = (
        (query_x[:, None] == key_x[None, :])
        & (query_y[:, None] == key_y[None, :])
        & (query_z[:, None] == key_z[None, :])
    )
    query_grid = queries.reshape(width_x, width_y, depth, local_heads, HD)
    upstream_grid = upstream.reshape(width_x, width_y, depth, local_heads, HD)
    pair_grid = pair_padded.reshape(key_span_x_full, key_span_y, depth, local_heads, 2, HD)

    def attend_block(block_index, carry):
        query_sums, pair_sums, outputs = carry
        first_row = block_index * block_x
        query_block = lax.dynamic_slice_in_dim(query_grid, first_row, block_x, 0).reshape(
            query_rows, local_heads, HD
        )
        upstream_block = lax.dynamic_slice_in_dim(upstream_grid, first_row, block_x, 0).reshape(
            query_rows, local_heads, HD
        )
        pair_block = lax.dynamic_slice_in_dim(pair_grid, first_row, key_span_x, 0).reshape(
            key_rows, local_heads, 2, HD
        )
        keys_block = pair_block[:, :, 0, :]
        values_block = pair_block[:, :, 1, :]
        live_keys = (
            lax.dynamic_slice_in_dim(valid_padded, first_row, key_span_x, 0).reshape(key_rows) > 0
        )
        allowed = within & (live_keys[None, :] | self_pair)
        scores = (
            jnp.einsum("qhe,khe->hqk", query_block, keys_block, preferred_element_type=jnp.float32)
            * score_scale
        )
        scores = jnp.where(allowed[None], scores, -jnp.inf)
        row_max = jnp.max(scores, axis=-1, keepdims=True)
        raised = jnp.exp(scores - row_max)
        weights = (raised / jnp.sum(raised, axis=-1, keepdims=True)).astype(jnp.bfloat16)
        result = jnp.einsum(
            "hqk,khe->qhe", weights, values_block, preferred_element_type=jnp.float32
        )
        weight_gradient = jnp.einsum(
            "qhe,khe->hqk", upstream_block, values_block, preferred_element_type=jnp.float32
        )
        row_inner = jnp.sum(upstream_block.astype(jnp.float32) * result, axis=-1)
        score_gradient = (
            weights.astype(jnp.float32) * (weight_gradient - row_inner.T[:, :, None]) * score_scale
        ).astype(jnp.bfloat16)
        query_gradient = jnp.einsum(
            "hqk,khe->qhe", score_gradient, keys_block, preferred_element_type=jnp.float32
        )
        key_gradient = jnp.einsum(
            "hqk,qhe->khe", score_gradient, query_block, preferred_element_type=jnp.float32
        )
        value_gradient = jnp.einsum(
            "hqk,qhe->khe", weights, upstream_block, preferred_element_type=jnp.float32
        )
        pair_gradient = jnp.stack([key_gradient, value_gradient], axis=2).reshape(
            key_span_x, key_span_y, depth, local_heads * 2 * HD
        )
        query_sums = lax.dynamic_update_slice_in_dim(
            query_sums,
            query_gradient.reshape(block_x, width_y, depth, local_heads * HD),
            first_row,
            0,
        )
        previous = lax.dynamic_slice_in_dim(pair_sums, first_row, key_span_x, 0)
        pair_sums = lax.dynamic_update_slice_in_dim(
            pair_sums, previous + pair_gradient, first_row, 0
        )
        outputs = lax.dynamic_update_slice_in_dim(
            outputs,
            result.astype(jnp.bfloat16).reshape(block_x, width_y, depth, local_heads * HD),
            first_row,
            0,
        )
        return (query_sums, pair_sums, outputs)

    start = (
        jnp.zeros((width_x, width_y, depth, local_heads * HD), jnp.float32),
        jnp.zeros((key_span_x_full, key_span_y, depth, local_heads * 2 * HD), jnp.float32),
        jnp.zeros((width_x, width_y, depth, local_heads * HD), jnp.bfloat16),
    )
    query_sums, pair_sums, outputs = lax.fori_loop(0, block_count, attend_block, start)
    rims_first = jnp.concatenate([pair_sums[:REACH], pair_sums[width_x + REACH :]], axis=0)
    from_first = extended(rims_first.astype(jnp.bfloat16), (("gx", 0),), REACH).astype(
        rims_first.dtype
    )
    interior = pair_sums[REACH : width_x + REACH]
    interior = interior.at[:REACH].add(from_first[:REACH])
    interior = interior.at[width_x - REACH :].add(from_first[3 * REACH :])
    rims_second = jnp.concatenate([interior[:, :REACH], interior[:, width_y + REACH :]], axis=1)
    from_second = extended(rims_second.astype(jnp.bfloat16), (("gy", 1),), REACH).astype(
        rims_second.dtype
    )
    centre = interior[:, REACH : width_y + REACH]
    centre = centre.at[:, :REACH].add(from_second[:, :REACH])
    centre = centre.at[:, width_y - REACH :].add(from_second[:, 3 * REACH :])
    query_part = query_sums.reshape(token_count, local_heads, 1, HD)
    pair_part = centre.reshape(token_count, local_heads, 2, HD)
    dprojected = (
        jnp.concatenate([query_part, pair_part], axis=2)
        .reshape(token_count, local_heads * 3 * HD)
        .astype(jnp.bfloat16)
    )
    partial_terms = jnp.einsum(
        "nc,dc->nd", dprojected, input_weight, preferred_element_type=jnp.float32
    ).reshape(width_x, width_y, depth, model_width)
    token_gradient = lax.psum_scatter(partial_terms, "ha", scatter_dimension=3, tiled=True).astype(
        jnp.bfloat16
    )
    attended_flat = outputs.reshape(token_count, local_heads * HD)
    part_input = jnp.einsum(
        "nd,nc->dc", flat_tokens, dprojected, preferred_element_type=jnp.float32
    )
    part_output = jnp.einsum(
        "ne,nd->ed", attended_flat, flat_cotangent, preferred_element_type=jnp.float32
    )
    summed_input, summed_output = (
        lax.psum(part_input.astype(jnp.bfloat16), ("gx", "gy")).astype(jnp.float32),
        lax.psum(part_output.astype(jnp.bfloat16), ("gx", "gy")).astype(jnp.float32),
    )
    normaliser = (token_count * lax.axis_size("gx") * lax.axis_size("gy")) ** (-0.5)
    return (token_gradient, summed_input * normaliser, summed_output * normaliser)


def solution(mesh):
    placed = (
        P("gx", "gy", None, None),
        P(None, "ha"),
        P("ha", None),
        P("gx", "gy"),
        P("gx", "gy", None, None),
    )
    return jax.shard_map(
        shards,
        mesh=mesh,
        in_specs=placed,
        out_specs=(P("gx", "gy", None, "ha"), P(None, "ha"), P("ha", None)),
        check_vma=False,
    )
```

profile of v0, /device:TPU:0, one launch (start us, length us, event | category | flops | bytes accessed | tf_op | source)
XLA Modules:
  0.0 429.6 jit_solution(15858001204018962524)
XLA Ops:
  11.0 3.5 collective-permute-start.4
  24.8 5.9 %collective-permute-start = (bf16[3,16,16,128]{3,2,1,0:T(8,128)(2,1)}, bf16[3,16,16,128]{3,2,1,0:T(8,128)(2,1)}, u32[]{:S(2)}, u32[]{:S(2)}) collective-permute-start(bf16[3,16,16,128]{3,2,1,0:T(8,128)(2,1)} %slice.209), channel_id=1, source_target_pairs={{0,16},{16,32},{32,48},{48,64},{64,80},{80,96},{96,112},{1,17},{17... | collective-permute-start | bytes 589832 | tf_op jit(solution)/shard_map/ppermute | solution.py:15
  41.4 6.2 %collective-permute-start.2 = (bf16[14,3,16,128]{3,2,1,0:T(8,128)(2,1)S(1)}, bf16[14,3,16,128]{3,2,1,0:T(8,128)(2,1)S(1)}, u32[]{:S(2)}, u32[]{:S(2)}) collective-permute-start(bf16[14,3,16,128]{3,2,1,0:T(8,128)(2,1)S(1)} %get-tuple-element.401), channel_id=1, source_target_pairs={{0,4},{4,8},{8,12},{1,5},{5,9},{9,13},{2,6},{6,10},{10,14},{3,7},{... | collective-permute-start | bytes 516104 | tf_op jit(solution)/shard_map/ppermute | solution.py:15
  60.7 128.2 %while.23 = (s32[]{:T(128)}, bf16[8,16,16,64]{3,2,1,0:T(8,128)(2,1)}, f32[14,22,16,128]{3,2,1,0:T(8,128)}, bf16[8,16,16,64]{3,2,1,0:T(8,128)(2,1)}, bf16[14,22,1...) while((s32[]{:T(128)}, ...), condition=%wide.region_4.5_spmd.clone.clone, body=%wide.region_0.4_spmd.clone.clone.sunk | while | flops 1152845056 | bytes 82846784 | solution.py:152
  66.3 5.8 %fusion.85 = (f32[512]{0:T(512)S(1)}, f32[512,2816]{1,0:T(8,128)S(1)}) fusion(bf16[512,64]{1,0:T(8,128)(2,1)S(1)} %bitcast.150, bf16[2816,1,2,64]{3,0,2,1:T(8,128)(2,1)S(1)} %bitcast.143, pred[2816]{0:T(1024)(128)(4,1)S(1)} %gt.22, s32[2816]{0:T(1024)S(1)} %get-tuple-element.564, s32[512]{0:T(512)S(1)} %get-tuple-element.565, ...), kind=kOutput, calls=%fused_computation.123.clone.1 | convolution fusion | flops 214826496 | bytes 6667264 | tf_op jit(solution)/shard_map/while/body/eval_jaxpr/qhe,khe->hqk/dot_general | solution.py:100
  83.6 3.3 copy.74
  86.9 3.2 reshape.514
  98.4 5.8 %fusion.85 = (f32[512]{0:T(512)S(1)}, f32[512,2816]{1,0:T(8,128)S(1)}) fusion(bf16[512,64]{1,0:T(8,128)(2,1)S(1)} %bitcast.150, bf16[2816,1,2,64]{3,0,2,1:T(8,128)(2,1)S(1)} %bitcast.143, pred[2816]{0:T(1024)(128)(4,1)S(1)} %gt.22, s32[2816]{0:T(1024)S(1)} %get-tuple-element.564, s32[512]{0:T(512)S(1)} %get-tuple-element.565, ...), kind=kOutput, calls=%fused_computation.123.clone.1 | convolution fusion | flops 214826496 | bytes 6667264 | tf_op jit(solution)/shard_map/while/body/eval_jaxpr/qhe,khe->hqk/dot_general | solution.py:100
  115.7 3.3 copy.74
  119.0 3.2 reshape.514
  130.4 5.8 %fusion.85 = (f32[512]{0:T(512)S(1)}, f32[512,2816]{1,0:T(8,128)S(1)}) fusion(bf16[512,64]{1,0:T(8,128)(2,1)S(1)} %bitcast.150, bf16[2816,1,2,64]{3,0,2,1:T(8,128)(2,1)S(1)} %bitcast.143, pred[2816]{0:T(1024)(128)(4,1)S(1)} %gt.22, s32[2816]{0:T(1024)S(1)} %get-tuple-element.564, s32[512]{0:T(512)S(1)} %get-tuple-element.565, ...), kind=kOutput, calls=%fused_computation.123.clone.1 | convolution fusion | flops 214826496 | bytes 6667264 | tf_op jit(solution)/shard_map/while/body/eval_jaxpr/qhe,khe->hqk/dot_general | solution.py:100
  147.8 3.3 copy.74
  151.0 3.2 reshape.514
  162.5 5.8 %fusion.85 = (f32[512]{0:T(512)S(1)}, f32[512,2816]{1,0:T(8,128)S(1)}) fusion(bf16[512,64]{1,0:T(8,128)(2,1)S(1)} %bitcast.150, bf16[2816,1,2,64]{3,0,2,1:T(8,128)(2,1)S(1)} %bitcast.143, pred[2816]{0:T(1024)(128)(4,1)S(1)} %gt.22, s32[2816]{0:T(1024)S(1)} %get-tuple-element.564, s32[512]{0:T(512)S(1)} %get-tuple-element.565, ...), kind=kOutput, calls=%fused_computation.123.clone.1 | convolution fusion | flops 214826496 | bytes 6667264 | tf_op jit(solution)/shard_map/while/body/eval_jaxpr/qhe,khe->hqk/dot_general | solution.py:100
  179.8 3.3 copy.74
  191.0 3.6 collective-permute-start.8
  198.5 7.3 %collective-permute-done.9 = bf16[3,22,16,128]{3,2,1,0:T(8,128)(2,1)S(1)} collective-permute-done((bf16[3,22,16,128]{3,2,1,0:T(8,128)(2,1)S(1)}, bf16[3,22,16,128]{3,2,1,0:T(8,128)(2,1)S(1)}, u32[]{:S(2)}, u32[]{:S(2)}) %collective-permute-start.9) | collective-permute-done | bytes 270368 | tf_op jit(solution)/shard_map/ppermute | solution.py:18
  206.8 6.8 %collective-permute-start.10 = (bf16[8,3,16,128]{3,2,1,0:T(8,128)(2,1)}, bf16[8,3,16,128]{3,2,1,0:T(8,128)(2,1)}, u32[]{:S(2)}, u32[]{:S(2)}) collective-permute-start(bf16[8,3,16,128]{3,2,1,0:T(8,128)(2,1)} %get-tuple-element.405), channel_id=1, source_target_pairs={{0,4},{4,8},{8,12},{1,5},{5,9},{9,13},{2,6},{6,10},{10,14},{3,7},{... | collective-permute-start | bytes 294920 | tf_op jit(solution)/shard_map/ppermute | solution.py:15
  230.4 4.1 convert_element_type.112
  236.9 20.4 %copy.58 = f32[8,16,16,384]{2,1,0,3:T(8,128)} copy(f32[8,16,16,384]{3,2,1,0:T(8,128)} %fusion.14) | data formatting | bytes 6291456
  257.2 21.8 %reshape.511 = f32[384,2048]{1,0:T(8,128)} reshape(f32[384,8,16,16]{3,2,1,0:T(8,128)} %bitcast.147) | data formatting | bytes 6291456
  281.9 128.5 %psum.15 = bf16[64,384]{1,0:T(8,128)(2,1)S(1)} all-reduce(bf16[64,384]{1,0:T(8,128)(2,1)S(1)} %fusion.9), channel_id=1, replica_groups=mesh['gx'=8,'gy'=4,'ha'=4] {'gx','gy'}, use_global_device_ids=true, to_apply=%region_7.8 | all-reduce | flops 24576 | bytes 98304 | tf_op jit(solution)/shard_map/psum | solution.py:189
  412.7 4.7 %reshape.512 = bf16[96,8,16,16]{3,2,1,0:T(8,128)(2,1)} reshape(f32[96,2048]{1,0:T(8,128)} %reduce-scatter.4.cloned.1.call-done) | data formatting | bytes 1179648
  417.4 4.8 %copy.59 = bf16[8,16,16,96]{3,2,1,0:T(8,128)(2,1)} copy(bf16[8,16,16,96]{2,1,0,3:T(8,128)(2,1)} %bitcast.154) | data formatting | bytes 786432
  (197 shorter events, 150.0 us)
Async XLA Ops:
  8.0 7.8 %copy-start = (bf16[8,16,16,384]{3,2,1,0:T(8,128)(2,1)S(1)}, bf16[8,16,16,384]{3,2,1,0:T(8,128)(2,1)}, u32[]{:S(2)}) copy-start(bf16[8,16,16,384]{3,2,1,0:T(8,128)(2,1)} %param.15) | copy-start | bytes 4718596
  8.0 403.1 %all-reduce.2.cloned.1.call-start = ((), (), s32[]{:S(2)}) async-start(), calls=%async_computation.1 | async-start | bytes 294912 | tf_op jit(solution)/shard_map/psum | solution.py:188
  10.3 5.4 %copy-start.11 = (bf16[8,16,16]{2,1,0:T(8,128)(2,1)}, bf16[8,16,16]{2,1,0:T(8,128)(2,1)S(1)}, u32[]{:S(2)}) copy-start(bf16[8,16,16]{2,1,0:T(8,128)(2,1)S(1)} %fusion.17) | copy-start | bytes 12292
  11.0 24.1 %collective-permute-start.4 = (bf16[3,16,16]{2,1,0:T(8,128)(2,1)}, bf16[3,16,16]{2,1,0:T(8,128)(2,1)S(1)}, u32[]{:S(2)}, u32[]{:S(2)}) collective-permute-start(bf16[3,16,16]{2,1,0:T(8,128)(2,1)} %get-tuple-element.409), channel_id=1, source_target_pairs={{0,16},{16,32},{32,48},{48,64},{64,80},{80,96},{96,112},{1,17},{17... | collective-permute-start | bytes 4616 | tf_op jit(solution)/shard_map/ppermute | solution.py:15
  14.5 20.6 %collective-permute-start.5 = (bf16[3,16,16]{2,1,0:T(8,128)(2,1)}, bf16[3,16,16]{2,1,0:T(8,128)(2,1)}, u32[]{:S(2)}, u32[]{:S(2)}) collective-permute-start(bf16[3,16,16]{2,1,0:T(8,128)(2,1)} %get-tuple-element.410), channel_id=1, source_target_pairs={{16,0},{32,16},{48,32},{64,48},{80,64},{96,80},{112,96},{17,1},{33... | collective-permute-start | bytes 4616 | tf_op jit(solution)/shard_map/ppermute | solution.py:18
  15.8 15.5 %copy-start.4 = (bf16[8,16,16,384]{3,2,1,0:T(8,128)(2,1)S(1)}, bf16[8,16,16,384]{3,2,1,0:T(8,128)(2,1)}, u32[]{:S(2)}) copy-start(bf16[8,16,16,384]{3,2,1,0:T(8,128)(2,1)} %param.19) | copy-start | bytes 4718596
  21.4 18.1 %collective-permute-start.1 = (bf16[3,16,16,128]{3,2,1,0:T(8,128)(2,1)}, bf16[3,16,16,128]{3,2,1,0:T(8,128)(2,1)}, u32[]{:S(2)}, u32[]{:S(2)}) collective-permute-start(bf16[3,16,16,128]{3,2,1,0:T(8,128)(2,1)} %slice.212), channel_id=1, source_target_pairs={{16,0},{32,16},{48,32},{64,48},{80,64},{96,80},{112,96},{17,1},{33... | collective-permute-start | bytes 589832 | tf_op jit(solution)/shard_map/ppermute | solution.py:18
  24.8 13.6 %collective-permute-start = (bf16[3,16,16,128]{3,2,1,0:T(8,128)(2,1)}, bf16[3,16,16,128]{3,2,1,0:T(8,128)(2,1)}, u32[]{:S(2)}, u32[]{:S(2)}) collective-permute-start(bf16[3,16,16,128]{3,2,1,0:T(8,128)(2,1)} %slice.209), channel_id=1, source_target_pairs={{0,16},{16,32},{32,48},{48,64},{64,80},{80,96},{96,112},{1,17},{17... | collective-permute-start | bytes 589832 | tf_op jit(solution)/shard_map/ppermute | solution.py:15
  35.8 16.2 %collective-permute-start.6 = (bf16[14,3,16]{2,1,0:T(4,128)(2,1)S(1)}, bf16[14,3,16]{2,1,0:T(4,128)(2,1)S(1)}, u32[]{:S(2)}, u32[]{:S(2)}) collective-permute-start(bf16[14,3,16]{2,1,0:T(4,128)(2,1)S(1)} %get-tuple-element.407), channel_id=1, source_target_pairs={{0,4},{4,8},{8,12},{1,5},{5,9},{9,13},{2,6},{6,10},{10,14},{3,7},{... | collective-permute-start | bytes 4040 | tf_op jit(solution)/shard_map/ppermute | solution.py:15
  37.1 14.9 %collective-permute-start.7 = (bf16[14,3,16]{2,1,0:T(4,128)(2,1)S(1)}, bf16[14,3,16]{2,1,0:T(4,128)(2,1)S(1)}, u32[]{:S(2)}, u32[]{:S(2)}) collective-permute-start(bf16[14,3,16]{2,1,0:T(4,128)(2,1)S(1)} %get-tuple-element.408), channel_id=1, source_target_pairs={{4,0},{8,4},{12,8},{5,1},{9,5},{13,9},{6,2},{10,6},{14,10},{7,3},{... | collective-permute-start | bytes 4040 | tf_op jit(solution)/shard_map/ppermute | solution.py:18
  41.4 12.0 %collective-permute-start.2 = (bf16[14,3,16,128]{3,2,1,0:T(8,128)(2,1)S(1)}, bf16[14,3,16,128]{3,2,1,0:T(8,128)(2,1)S(1)}, u32[]{:S(2)}, u32[]{:S(2)}) collective-permute-start(bf16[14,3,16,128]{3,2,1,0:T(8,128)(2,1)S(1)} %get-tuple-element.401), channel_id=1, source_target_pairs={{0,4},{4,8},{8,12},{1,5},{5,9},{9,13},{2,6},{6,10},{10,14},{3,7},{... | collective-permute-start | bytes 516104 | tf_op jit(solution)/shard_map/ppermute | solution.py:15
  47.5 6.2 %collective-permute-start.3 = (bf16[14,3,16,128]{3,2,1,0:T(8,128)(2,1)S(1)}, bf16[14,3,16,128]{3,2,1,0:T(8,128)(2,1)}, u32[]{:S(2)}, u32[]{:S(2)}) collective-permute-start(bf16[14,3,16,128]{3,2,1,0:T(8,128)(2,1)S(1)} %get-tuple-element.402), channel_id=1, source_target_pairs={{4,0},{8,4},{12,8},{5,1},{9,5},{13,9},{6,2},{10,6},{14,10},{7,3},{... | collective-permute-start | bytes 516104 | tf_op jit(solution)/shard_map/ppermute | solution.py:18
  57.2 3.5 copy-start.13
  77.2 2.7 copy-start.2
  109.3 2.7 copy-start.2
  188.9 7.0 %copy-start.3 = (f32[14,22,16,128]{3,2,1,0:T(8,128)S(1)}, f32[14,22,16,128]{3,2,1,0:T(8,128)}, u32[]{:S(2)}) copy-start(f32[14,22,16,128]{3,2,1,0:T(8,128)} %get-tuple-element.223) | copy-start | bytes 7569412
  191.0 7.5 %collective-permute-start.8 = (bf16[3,22,16,128]{3,2,1,0:T(8,128)(2,1)S(1)}, bf16[3,22,16,128]{3,2,1,0:T(8,128)(2,1)S(1)}, u32[]{:S(2)}, u32[]{:S(2)}) collective-permute-start(bf16[3,22,16,128]{3,2,1,0:T(8,128)(2,1)S(1)} %get-tuple-element.399), channel_id=1, source_target_pairs={{0,16},{16,32},{32,48},{48,64},{64,80},{80,96},{96,112},{1,17},{17... | collective-permute-start | bytes 811016 | tf_op jit(solution)/shard_map/ppermute | solution.py:15
  194.6 11.3 %collective-permute-start.9 = (bf16[3,22,16,128]{3,2,1,0:T(8,128)(2,1)S(1)}, bf16[3,22,16,128]{3,2,1,0:T(8,128)(2,1)S(1)}, u32[]{:S(2)}, u32[]{:S(2)}) collective-permute-start(bf16[3,22,16,128]{3,2,1,0:T(8,128)(2,1)S(1)} %get-tuple-element.400), channel_id=1, source_target_pairs={{16,0},{32,16},{48,32},{64,48},{80,64},{96,80},{112,96},{17,1},{33... | collective-permute-start | bytes 811016 | tf_op jit(solution)/shard_map/ppermute | solution.py:18
  205.9 9.0 %copy-start.8 = (bf16[8,16,16,64]{3,2,1,0:T(8,128)(2,1)S(1)}, bf16[8,16,16,64]{3,2,1,0:T(8,128)(2,1)}, u32[]{:S(2)}) copy-start(bf16[8,16,16,64]{3,2,1,0:T(8,128)(2,1)} %get-tuple-element.222) | copy-start | bytes 786436
  206.8 10.1 %collective-permute-start.10 = (bf16[8,3,16,128]{3,2,1,0:T(8,128)(2,1)}, bf16[8,3,16,128]{3,2,1,0:T(8,128)(2,1)}, u32[]{:S(2)}, u32[]{:S(2)}) collective-permute-start(bf16[8,3,16,128]{3,2,1,0:T(8,128)(2,1)} %get-tuple-element.405), channel_id=1, source_target_pairs={{0,4},{4,8},{8,12},{1,5},{5,9},{9,13},{2,6},{6,10},{10,14},{3,7},{... | collective-permute-start | bytes 294920 | tf_op jit(solution)/shard_map/ppermute | solution.py:15
  213.6 6.3 %collective-permute-start.11 = (bf16[8,3,16,128]{3,2,1,0:T(8,128)(2,1)}, bf16[8,3,16,128]{3,2,1,0:T(8,128)(2,1)}, u32[]{:S(2)}, u32[]{:S(2)}) collective-permute-start(bf16[8,3,16,128]{3,2,1,0:T(8,128)(2,1)} %get-tuple-element.406), channel_id=1, source_target_pairs={{4,0},{8,4},{12,8},{5,1},{9,5},{13,9},{6,2},{10,6},{14,10},{7,3},{... | collective-permute-start | bytes 294920 | tf_op jit(solution)/shard_map/ppermute | solution.py:18
  216.9 9.6 %copy-start.9 = (bf16[2048,1,1,64]{0,3,2,1:T(8,128)(2,1)S(1)}, bf16[2048,1,1,64]{0,3,2,1:T(8,128)(2,1)}, u32[]{:S(2)}) copy-start(bf16[2048,1,1,64]{0,3,2,1:T(8,128)(2,1)} %copy.53) | copy-start | bytes 786436
  229.1 5.4 %copy-start.10 = (bf16[384,192]{0,1:T(8,128)(2,1)S(1)}, bf16[384,192]{0,1:T(8,128)(2,1)}, u32[]{:S(2)}) copy-start(bf16[384,192]{0,1:T(8,128)(2,1)} %param.16) | copy-start | bytes 442372
  230.3 182.4 %reduce-scatter.4.cloned.1.call-start = ((), (), s32[]{:S(2)}) async-start(), calls=%async_computation.2 | async-start | bytes 3932160
  (10 other events, 17.2 us)
Sparse Core Ops, SparseCore 0:
  230.5 102.9 all-reduce.1
Sparse Core Ops, SparseCore 1:
  279.2 42.6 reduce-scatter.3
where the time goes:
time: 432 us; the launch traced here: 430 us
  local copies, waits for them, and re-layouts  141 us (33%)
  blocking collectives  129 us (30%)
  matrix products  57 us (13%)
  other arithmetic  38.5 us (9%)
  starting transfers between devices  35 us (8%)
  between operations  15.9 us (4%)
  waiting for transfers between devices  13.2 us (3%)
    psum x1, blocking collectives, shards(): lax.psum(part_output.astype(jnp.bfloat16), ('gx', 'gy')).astype(jnp.float32)  129 us
    unnamed x34, local copies, waits for them, and re-layouts  60.2 us
    ppermute x6, starting transfers between devices, extended(): lax.ppermute(lax.slice_in_dim(block, block.shape[dim] - width, None, axis...  27.2 us
    dot_general x4, matrix products, attend_block(): jnp.einsum('qhe,khe->hqk', query_block, keys_block, preferred_element_typ...  23.3 us
    another operation x4, local copies, waits for them, and re-layouts, attend_block(): jnp.stack([key_gradient, value_gradient], axis=2)  13.1 us
    reshape x4, local copies, waits for them, and re-layouts, attend_block(): jnp.stack([key_gradient, value_gradient], axis=2)  12.6 us
    dynamic_update_slice x4, other arithmetic, attend_block(): lax.dynamic_update_slice_in_dim(pair_sums, previous + pair_gradient, firs...  10.7 us
    ppermute x6, waiting for transfers between devices, extended(): lax.ppermute(lax.slice_in_dim(block, 0, width, axis=dim), axis, backward)  10.7 us
  transfers between devices with their start and end apart: 14, of which 4 were waited for; matrix products, arithmetic and copies ran while one was open for 17% of the time, Pallas kernels for 0%

commit v1 on v0

v1 whole, which is shorter than its diff:
```python
import jax
import jax.numpy as jnp
from jax import lax
from jax.experimental import pallas as pl
from jax.experimental.pallas import tpu as pltpu
from jax.sharding import PartitionSpec as P

HD = 64
REACH = 3
LANES = 128
BLOCK = 4
SPAN = BLOCK + 2 * REACH
BIG = 2.0**100
F32 = jnp.float32
BF16 = jnp.bfloat16
LANE_X = 64
LANE_Y = 72
LANE_Z = 88
LANE_F = 104

SIDES = ((-1, 0), (1, 0), (0, -1), (0, 1), (-1, -1), (-1, 1), (1, -1), (1, 1))


def dot(a, b):
    return lax.dot_general(a, b, (((1,), (0,)), ((), ())), preferred_element_type=F32)


def dot_t(a, b):
    return lax.dot_general(a, b, (((1,), (1,)), ((), ())), preferred_element_type=F32)


def edge(step, extent):
    if step < 0:
        return 0, REACH
    if step > 0:
        return extent - REACH, extent
    return 0, extent


def halo(step, extent):
    if step < 0:
        return 0, REACH
    if step > 0:
        return extent + REACH, extent + 2 * REACH
    return REACH, extent + REACH


def project_kernel(tok, cot, w, wo, bits, kv_o, qu_o, flags_o, *sends):
    nx, ny, nz, _ = kv_o.shape
    model = tok.shape[-1]
    weight = w[...]
    wide = jnp.concatenate(
        [weight[:, HD:], weight[:, :HD], jnp.zeros((model, HD), BF16)], axis=1
    )
    out_w = jnp.concatenate([jnp.zeros((HD, model), BF16), wo[...]], axis=0)
    z = lax.broadcasted_iota(jnp.int32, (nz, LANES), 0)
    flags = (lax.shift_right_logical(jnp.broadcast_to(bits[...], (nz, LANES)), z) & 1).astype(F32)
    flags = flags.astype(BF16)
    flags_o[...] = flags
    rows = ny * nz
    for x in range(nx):
        part = dot(tok[x * rows : (x + 1) * rows, :], wide)
        ups = dot_t(cot[x * rows : (x + 1) * rows, :], out_w)
        kv_o[x] = part[:, :LANES].astype(BF16).reshape(ny, nz, LANES)
        qu_o[x] = (part[:, LANES:] + ups).astype(BF16).reshape(ny, nz, LANES)
    for (sx, sy), out in zip(SIDES, sends):
        x0, x1 = edge(sx, nx)
        y0, y1 = edge(sy, ny)
        n = y1 - y0
        for x in range(x0, x1):
            out[(x - x0) * n : (x - x0 + 1) * n] = kv_o[x, y0:y1]
        out[(x1 - x0) * n] = flags


def attend_kernel(kv, qu, flags, *refs):
    recvs, refs = refs[:8], refs[8:]
    qa_o, dkv_o = refs[:2]
    backs, refs = refs[2:10], refs[10:]
    kvx, kaug, dkv, s_scr, p_scr, d_scr = refs
    nx, ny, nz, _ = kv.shape
    wx, wy = nx + 2 * REACH, ny + 2 * REACH

    lane = lax.broadcasted_iota(jnp.int32, (nz, LANES), 1)
    zrow = lax.broadcasted_iota(jnp.int32, (nz, LANES), 0)
    low = lane < HD
    far_z = (lane >= LANE_Z) & (lane < LANE_Z + nz) & (jnp.abs(lane - LANE_Z - zrow) > REACH)
    base_z = jnp.where(far_z, -BIG, 0.0).astype(F32)

    def base_of(first, extent, at):
        mine = (lane >= first) & (lane < first + extent)
        return jnp.where(mine & (jnp.abs(lane - first - (at - REACH)) > REACH), -BIG, 0.0)

    base_x = [base_of(LANE_X, nx, x) for x in range(wx)]
    base_y = [base_of(LANE_Y, ny, y) + base_z for y in range(wy)]

    def place(source, group, flag, sy, kx, ky):
        tile = source[group] if isinstance(group, int) else source[group[0], group[1]]
        kvx[kx, ky] = tile
        bias = base_x[kx] + base_y[ky] + jnp.where(lane == LANE_F + sy, flag, 0.0)
        kaug[kx, ky] = jnp.where(low, tile, bias.astype(BF16))

    def rolled(tile, x):
        shift = (LANE_F - x * ny) % LANES
        value = (tile.astype(F32) - 1.0) * BIG
        return pltpu.roll(value, shift, 1) if shift else value

    own = flags[...]
    for x in range(nx):
        plane = rolled(own, x)
        for y in range(ny):
            place(kv, (x, y), plane, y, x + REACH, y + REACH)
    for (sx, sy), piece in zip(SIDES, recvs):
        x0, x1 = edge(sx, nx)
        y0, y1 = edge(sy, ny)
        n = y1 - y0
        hx = halo(-sx, nx)[0]
        hy = halo(-sy, ny)[0]
        tile = piece[(x1 - x0) * n]
        for x in range(x0, x1):
            plane = rolled(tile, x)
            for y in range(y0, y1):
                place(piece, (x - x0) * n + y - y0, plane, y, hx + x - x0, hy + y - y0)

    dkv[...] = jnp.zeros(dkv.shape, F32)
    rows = BLOCK * BLOCK * nz
    keys = SPAN * nz
    qlane = lax.broadcasted_iota(jnp.int32, (rows, LANES), 1)
    qrow = lax.broadcasted_iota(jnp.int32, (rows, LANES), 0)
    strip = BLOCK * nz
    drow = lax.broadcasted_iota(jnp.int32, (strip, rows), 0)
    dlane = lax.broadcasted_iota(jnp.int32, (strip, rows), 1)
    blocks_y = ny // BLOCK
    scale = HD ** (-0.5)

    def one(index, carry):
        x0 = index // blocks_y * BLOCK
        y0 = index % blocks_y * BLOCK
        both = qu[pl.ds(x0, BLOCK), pl.ds(y0, BLOCK)].reshape(rows, LANES)
        qx = x0 + qrow // strip
        qy = y0 + qrow // nz % BLOCK
        hot = (
            (qlane == LANE_X + qx)
            | (qlane == LANE_Y + qy)
            | (qlane == LANE_Z + qrow % nz)
            | ((qlane >= LANE_F) & (qlane < LANE_F + ny))
        )
        wide = both.astype(F32)
        qlow = qlane < HD
        scaled = jnp.where(qlow, wide * scale, 0.0)
        ups = jnp.where(qlow, 0.0, wide)
        aug = jnp.where(qlow, scaled, jnp.where(hot, 1.0, 0.0))
        aug_t = aug.T.astype(BF16)
        q_t = scaled.T.astype(BF16)
        u_t32 = ups.T
        u_t = u_t32.astype(BF16)
        mixed = jnp.concatenate([scaled.astype(BF16), ups.astype(BF16)], axis=0)

        top = jnp.full((8, rows), -jnp.inf, F32)
        for j in range(SPAN):
            s = dot(kaug[x0 + j, pl.ds(y0, SPAN)].reshape(keys, LANES), aug_t)
            if REACH <= j < REACH + BLOCK:
                mid = kvx[x0 + j, pl.ds(y0 + REACH, BLOCK)].reshape(strip, LANES)
                plain = dot(mid, q_t)
                diagonal = dlane - (j - REACH) * strip == drow
                a, b = REACH * nz, REACH * nz + strip
                s = jnp.concatenate([s[:a], jnp.where(diagonal, plain, s[a:b]), s[b:]], axis=0)
            s_scr[j] = s
            top = jnp.maximum(top, jnp.max(s.reshape(keys // 8, 8, rows), axis=0))
        top = jnp.max(top, axis=0, keepdims=True)
        total = jnp.zeros((8, rows), F32)
        for j in range(SPAN):
            e = jnp.exp(s_scr[j] - top)
            s_scr[j] = e
            total = total + jnp.sum(e.reshape(keys // 8, 8, rows), axis=0)
        inverse = 1.0 / jnp.sum(total, axis=0, keepdims=True)
        for j in range(SPAN):
            p_scr[j * keys : (j + 1) * keys] = (s_scr[j] * inverse).astype(BF16)
        block = kvx[pl.ds(x0, SPAN), pl.ds(y0, SPAN)].reshape(SPAN * keys, LANES)
        block_t = block.T
        o_t = dot(block_t[HD:], p_scr[...])
        r = jnp.sum(u_t32[HD:] * o_t, axis=0, keepdims=True)
        for j in range(SPAN):
            kvj = kvx[x0 + j, pl.ds(y0, SPAN)].reshape(keys, LANES)
            g = dot(kvj, u_t)
            p = p_scr[j * keys : (j + 1) * keys]
            ds = (p.astype(F32) * (g - r)).astype(BF16)
            d_scr[j * keys : (j + 1) * keys] = ds
            both_grad = dot(jnp.concatenate([ds, p], axis=1), mixed)
            dkv[x0 + j, pl.ds(y0, SPAN)] += both_grad.reshape(SPAN, nz, LANES)
        q_grad = dot(block_t[:HD], d_scr[...]) * scale
        result = jnp.concatenate([q_grad, o_t], axis=0).T
        qa_o[pl.ds(x0, BLOCK), pl.ds(y0, BLOCK)] = result.astype(BF16).reshape(
            BLOCK, BLOCK, nz, LANES
        )
        return carry

    lax.fori_loop(0, (nx // BLOCK) * blocks_y, one, 0)

    for x in range(nx):
        dkv_o[x] = dkv[x + REACH, REACH : REACH + ny]
    for (sx, sy), out in zip(SIDES, backs):
        x0, x1 = halo(sx, nx)
        y0, y1 = halo(sy, ny)
        n = y1 - y0
        for x in range(x0, x1):
            out[(x - x0) * n : (x - x0 + 1) * n] = dkv[x, y0:y1].astype(BF16)


def tail_kernel(place, qa, dkv, tok, cot, w, *refs):
    recvs, refs = refs[:8], refs[8:]
    own_o, sends, sums_o, acc, grads = refs[0], refs[1:-3], refs[-3], refs[-2], refs[-1]
    nx, ny, nz, _ = dkv.shape
    acc[...] = dkv[...]
    for (sx, sy), piece in zip(SIDES, recvs):
        x0, x1 = edge(-sx, nx)
        y0, y1 = edge(-sy, ny)
        n = y1 - y0
        for x in range(x0, x1):
            acc[x, y0:y1] += piece[(x - x0) * n : (x - x0 + 1) * n].astype(F32)
    rows = nx * ny * nz
    grads[:, :LANES] = acc[...].reshape(rows, LANES).astype(BF16)
    grads[:, LANES:] = qa[...].reshape(rows, LANES)
    parts = w.shape[0]
    mine = place[0]

    def share(step):
        chunk = w[lax.rem(mine + step, parts)]
        wide = jnp.concatenate(
            [chunk[:, HD:], chunk[:, :HD], jnp.zeros((chunk.shape[0], HD), BF16)], axis=1
        )
        return dot_t(grads[...], wide)

    for step in range(1, parts):
        sends[step - 1][...] = share(step).astype(BF16)
    own_o[...] = share(0)
    grads_t = grads[...].T
    sums_o[: 3 * HD] = dot(grads_t[: 3 * HD], tok[...]).astype(BF16)
    sums_o[3 * HD :] = dot(grads_t[3 * HD :], cot[...]).astype(BF16)


def moved(pieces, reverse):
    nx, ny = lax.axis_size("gx"), lax.axis_size("gy")
    out = []
    for (sx, sy), piece in zip(SIDES, pieces):
        pairs = []
        for x in range(nx):
            for y in range(ny):
                if 0 <= x + sx < nx and 0 <= y + sy < ny:
                    pairs.append((x * ny + y, (x + sx) * ny + y + sy))
        out.append(lax.ppermute(piece, ("gx", "gy"), pairs))
    return out


def call(kernel, outs, scratch=(), scalars=0, count=0):
    vmem = pl.BlockSpec(memory_space=pltpu.VMEM)
    smem = pl.BlockSpec(memory_space=pltpu.SMEM)
    return pl.pallas_call(
        kernel,
        out_shape=outs,
        in_specs=[smem] * scalars + [vmem] * (count - scalars),
        out_specs=[vmem] * len(outs),
        scratch_shapes=list(scratch),
        compiler_params=pltpu.CompilerParams(vmem_limit_bytes=56 << 20),
    )


def shards(tokens, input_weight, output_weight, tissue_bits, cotangent):
    nx, ny, nz, model = tokens.shape
    rows = nx * ny * nz
    wx, wy = nx + 2 * REACH, ny + 2 * REACH
    flat_tokens = tokens.reshape(rows, model)
    flat_cotangent = cotangent.reshape(rows, model)
    shape = jax.ShapeDtypeStruct
    sizes = []
    for sx, sy in SIDES:
        x0, x1 = edge(sx, nx)
        y0, y1 = edge(sy, ny)
        sizes.append((x1 - x0) * (y1 - y0))
    kv, qu, flags, *sends = call(
        project_kernel,
        [shape((nx, ny, nz, LANES), BF16)] * 2
        + [shape((nz, LANES), BF16)]
        + [shape((n + 1, nz, LANES), BF16) for n in sizes],
        count=5,
    )(flat_tokens, flat_cotangent, input_weight, output_weight, tissue_bits.reshape(1, nx * ny))
    recvs = moved(sends, False)
    span_rows = SPAN * SPAN * nz
    block_rows = BLOCK * BLOCK * nz
    qa, dkv, *backs = call(
        attend_kernel,
        [shape((nx, ny, nz, LANES), BF16), shape((nx, ny, nz, LANES), F32)]
        + [shape((n, nz, LANES), BF16) for n in sizes],
        scratch=[
            pltpu.VMEM((wx, wy, nz, LANES), BF16),
            pltpu.VMEM((wx, wy, nz, LANES), BF16),
            pltpu.VMEM((wx, wy, nz, LANES), F32),
            pltpu.VMEM((SPAN, SPAN * nz, block_rows), F32),
            pltpu.VMEM((span_rows, block_rows), BF16),
            pltpu.VMEM((span_rows, block_rows), BF16),
        ],
        count=11,
    )(kv, qu, flags, *recvs)
    returned = moved(backs, True)
    parts = lax.axis_size("ha")
    width = model // parts
    mine = lax.axis_index("ha").astype(jnp.int32).reshape(1)
    own, *rest = call(
        tail_kernel,
        [shape((rows, width), F32)]
        + [shape((rows, width), BF16)] * (parts - 1)
        + [shape((4 * HD, model), BF16)],
        scratch=[pltpu.VMEM((nx, ny, nz, LANES), F32), pltpu.VMEM((rows, 2 * LANES), BF16)],
        scalars=1,
        count=14,
    )(
        mine,
        qa,
        dkv,
        flat_tokens,
        flat_cotangent,
        input_weight.reshape(parts, width, 3 * HD),
        *returned,
    )
    shares, sums = rest[:-1], rest[-1]
    total = own
    for step, piece in zip(range(1, parts), shares):
        ring = [(i, (i + step) % parts) for i in range(parts)]
        total = total + lax.ppermute(piece, "ha", ring).astype(F32)
    token_gradient = total.astype(BF16).reshape(nx, ny, nz, width)
    grid = ("gx", "gy")
    members = lax.axis_size("gx") * lax.axis_size("gy")
    split = sums.reshape(members, 4 * HD // members, model)
    met = lax.all_to_all(split, grid, 0, 0, tiled=True)
    mean = jnp.sum(met.astype(F32), axis=0, keepdims=True).astype(BF16)
    spread = lax.all_to_all(jnp.broadcast_to(mean, split.shape), grid, 0, 0, tiled=True)
    normaliser = (rows * members) ** (-0.5)
    whole = spread.reshape(4 * HD, model).astype(F32) * normaliser
    input_gradient = jnp.concatenate([whole[2 * HD : 3 * HD], whole[: 2 * HD]], axis=0).T
    return token_gradient, input_gradient, whole[3 * HD :]


def solution(mesh):
    placed = (
        P("gx", "gy", None, None),
        P(None, "ha"),
        P("ha", None),
        P("gx", "gy"),
        P("gx", "gy", None, None),
    )
    return jax.shard_map(
        shards,
        mesh=mesh,
        in_specs=placed,
        out_specs=(P("gx", "gy", None, "ha"), P(None, "ha"), P("ha", None)),
        check_vma=False,
    )
```

time: 432 us -> 161 us (0.37)
  local copies, waits for them, and re-layouts: 141 us -> 5.83 us
  blocking collectives: 129 us -> 19.8 us
  matrix products: 57 us -> 0 us
  Pallas kernels: 0 us -> 39.5 us
  other arithmetic: 38.5 us -> 1.84 us
  starting transfers between devices: 35 us -> 59.3 us
  waiting for transfers between devices: 13.2 us -> 32.5 us
  between operations: 15.9 us -> 1 us
    psum x1 -> x0, blocking collectives: 129 us -> none  [shards(): lax.psum(part_output.astype(jnp.bfloat16), ('gx', 'gy')).astype(jnp.float32)]
    unnamed x34 -> x35, local copies, waits for them, and re-layouts: 60.2 us -> 3.22 us
    dot_general x29 -> x0, matrix products: 57 us -> none  [the longest x4 23.3 us: attend_block(): jnp.einsum('qhe,khe->hqk', query_block, keys_block, preferred_element_typ...]
    pallas_call x0 -> x3, Pallas kernels: none -> 39.5 us  [the longest x1 29.9 us: shards(): call(attend_kernel, [shape((nx, ny, nz, LANES), BF16), shape((nx, ny, nz,...]
    ppermute x12 -> x19, starting transfers between devices: 34.9 us -> 55.1 us  [the longest x16 49.2 us: moved(): out.append(lax.ppermute(piece, ('gx', 'gy'), pairs))]
    all_to_all x0 -> x1, blocking collectives: none -> 19.8 us  [shards(): met = lax.all_to_all(split, grid, 0, 0, tiled=True)]
    reshape x9 -> x1, local copies, waits for them, and re-layouts: 19.3 us -> 1.25 us  [shards(): tissue_bits.reshape(1, nx * ny)]
    dynamic_slice x16 -> x0, local copies, waits for them, and re-layouts: 18 us -> none  [the longest x8 10.7 us: attend_block(): lax.dynamic_slice_in_dim(pair_grid, first_row, key_span_x, 0)]
  transfers between devices with their start and end apart: 14 -> 20, of which waited for: 4 -> 7; matrix products, arithmetic and copies ran while one was open for 17% -> 1% of each run, Pallas kernels for 0% -> 0%
where the time goes in v1:
time: 161 us; the launch traced here: 160 us
  starting transfers between devices  59.3 us (37%)
  Pallas kernels  39.5 us (25%)
  waiting for transfers between devices  32.5 us (20%)
  blocking collectives  19.8 us (12%)
  local copies, waits for them, and re-layouts  5.83 us (4%)
  other arithmetic  1.84 us (1%)
    ppermute x16, starting transfers between devices, moved(): out.append(lax.ppermute(piece, ('gx', 'gy'), pairs))  49.2 us
    pallas_call x1, Pallas kernels, shards(): call(attend_kernel, [shape((nx, ny, nz, LANES), BF16), shape((nx, ny, nz,...  29.9 us
    all_to_all x1, blocking collectives, shards(): met = lax.all_to_all(split, grid, 0, 0, tiled=True)  19.8 us
    ppermute x3, waiting for transfers between devices, shards(): total = total + lax.ppermute(piece, 'ha', ring).astype(F32)  18.6 us
    ppermute x16, waiting for transfers between devices, moved(): out.append(lax.ppermute(piece, ('gx', 'gy'), pairs))  11.8 us
    ppermute x3, starting transfers between devices, shards(): total = total + lax.ppermute(piece, 'ha', ring).astype(F32)  5.9 us
    pallas_call x1, Pallas kernels, shards(): call(tail_kernel, [shape((rows, width), F32)] + [shape((rows, width), BF1...  5.21 us
    pallas_call x1, Pallas kernels, shards(): call(project_kernel, [shape((nx, ny, nz, LANES), BF16)] * 2 + [shape((nz,...  4.35 us
  transfers between devices with their start and end apart: 20, of which 7 were waited for; matrix products, arithmetic and copies ran while one was open for 1% of the time, Pallas kernels for 0%

profile of v1, /device:TPU:0, one launch (start us, length us, event | category | flops | bytes accessed | tf_op | source)
XLA Modules:
  0.0 159.7 jit_solution(521213082870881720)
XLA Ops:
  1.9 1.7 %copy.8.w = bf16[384,192]{1,0:T(8,128)(2,1)} copy(bf16[384,192]{0,1:T(8,128)(2,1)} %param.6) | data formatting | bytes 294912 | tf_op args[1]
  3.6 4.4 %shard_map.76 = (bf16[8,16,16,128]{3,2,1,0:T(8,128)(2,1)}, bf16[8,16,16,128]{3,2,1,0:T(8,128)(2,1)}, bf16[16,128]{1,0:T(8,128)(2,1)}, bf16[49,16,128]{2,1,0:T(8,...) custom-call(bf16[2048,384]{1,0:T(8,128)(2,1)} %bitcast.14, ...), custom_call_target="tpu_custom_call" | custom-call | tf_op jit(solution)/shard_map/pallas_call | solution.py:279
  8.0 1.3 collective-permute-start
  9.3 4.6 %collective-permute-start.1 = (bf16[49,16,128]{2,1,0:T(8,128)(2,1)}, bf16[49,16,128]{2,1,0:T(8,128)(2,1)S(1)}, u32[]{:S(2)}, u32[]{:S(2)}) collective-permute-start(bf16[49,16,128]{2,1,0:T(8,128)(2,1)} %get-tuple-element.33), channel_id=1, source_target_pairs={{0,16},{4,20},{8,24},{12,28},{16,32},{20,36},{24,40},{28,44},{32,4... | collective-permute-start | bytes 602120 | tf_op jit(solution)/shard_map/ppermute | solution.py:250
  13.8 1.3 collective-permute-start.4
  15.8 1.3 collective-permute-start.2
  17.1 3.4 %collective-permute-done.4.refs_4_ = bf16[10,16,128]{2,1,0:T(8,128)(2,1)S(1)} collective-permute-done((bf16[10,16,128]{2,1,0:T(8,128)(2,1)}, bf16[10,16,128]{2,1,0:T(8,128)(2,1)S(1)}, u32[]{:S(2)}, u32[]{:S(2)}) %collective-permute-start.4) | collective-permute-done | bytes 40992 | tf_op jit(solution)/shard_map/ppermute | solution.py:250
  20.5 2.9 %collective-permute-start.3 = (bf16[25,16,128]{2,1,0:T(8,128)(2,1)}, bf16[25,16,128]{2,1,0:T(8,128)(2,1)S(1)}, u32[]{:S(2)}, u32[]{:S(2)}) collective-permute-start(bf16[25,16,128]{2,1,0:T(8,128)(2,1)} %get-tuple-element.35), channel_id=1, source_target_pairs={{0,4},{4,8},{8,12},{16,20},{20,24},{24,28},{32,36},{36,40},{40,44}... | collective-permute-start | bytes 307208 | tf_op jit(solution)/shard_map/ppermute | solution.py:250
  24.1 10.4 %collective-permute-start.7 = (bf16[10,16,128]{2,1,0:T(8,128)(2,1)}, bf16[10,16,128]{2,1,0:T(8,128)(2,1)S(1)}, u32[]{:S(2)}, u32[]{:S(2)}) collective-permute-start(bf16[10,16,128]{2,1,0:T(8,128)(2,1)} %get-tuple-element.39), channel_id=1, source_target_pairs={{0,20},{4,24},{8,28},{16,36},{20,40},{24,44},{32,52},{36,56},{40,6... | collective-permute-start | bytes 122888 | tf_op jit(solution)/shard_map/ppermute | solution.py:250
  34.5 2.0 %collective-permute-done.7.refs_7_ = bf16[10,16,128]{2,1,0:T(8,128)(2,1)S(1)} collective-permute-done((bf16[10,16,128]{2,1,0:T(8,128)(2,1)}, bf16[10,16,128]{2,1,0:T(8,128)(2,1)S(1)}, u32[]{:S(2)}, u32[]{:S(2)}) %collective-permute-start.7) | collective-permute-done | bytes 40992 | tf_op jit(solution)/shard_map/ppermute | solution.py:250
  37.3 29.9 %shard_map.77 = (bf16[8,16,16,128]{3,2,1,0:T(8,128)(2,1)}, f32[8,16,16,128]{3,2,1,0:T(8,128)}, bf16[48,16,128]{2,1,0:T(8,128)(2,1)}, bf16[48,16,128]{2,1,0:T(8,1...) custom-call(bf16[8,16,16,128]{3,2,1,0:T(8,128)(2,1)} %get-tuple-elem, ...), custom_call_target="tpu_custom_call" | custom-call | tf_op jit(solution)/shard_map/pallas_call | solution.py:289
  68.5 8.7 %collective-permute-start.9 = (bf16[48,16,128]{2,1,0:T(8,128)(2,1)}, bf16[48,16,128]{2,1,0:T(8,128)(2,1)S(1)}, u32[]{:S(2)}, u32[]{:S(2)}) collective-permute-start(bf16[48,16,128]{2,1,0:T(8,128)(2,1)} %get-tuple-element.43), channel_id=1, source_target_pairs={{0,16},{4,20},{8,24},{12,28},{16,32},{20,36},{24,40},{28,44},{32,4... | collective-permute-start | bytes 589832 | tf_op jit(solution)/shard_map/ppermute | solution.py:250
  80.6 4.5 %collective-permute-done.12.refs_4_ = bf16[9,16,128]{2,1,0:T(8,128)(2,1)S(1)} collective-permute-done((bf16[9,16,128]{2,1,0:T(8,128)(2,1)}, bf16[9,16,128]{2,1,0:T(8,128)(2,1)S(1)}, u32[]{:S(2)}, u32[]{:S(2)}) %collective-permute-start.12) | collective-permute-done | bytes 36896 | tf_op jit(solution)/shard_map/ppermute | solution.py:250
  87.1 10.9 %collective-permute-start.15 = (bf16[9,16,128]{2,1,0:T(8,128)(2,1)}, bf16[9,16,128]{2,1,0:T(8,128)(2,1)S(1)}, u32[]{:S(2)}, u32[]{:S(2)}) collective-permute-start(bf16[9,16,128]{2,1,0:T(8,128)(2,1)} %get-tuple-element.49), channel_id=1, source_target_pairs={{0,20},{4,24},{8,28},{16,36},{20,40},{24,44},{32,52},{36,56},{40,6... | collective-permute-start | bytes 110600 | tf_op jit(solution)/shard_map/ppermute | solution.py:250
  97.9 1.9 %collective-permute-done.15.refs_7_ = bf16[9,16,128]{2,1,0:T(8,128)(2,1)S(1)} collective-permute-done((bf16[9,16,128]{2,1,0:T(8,128)(2,1)}, bf16[9,16,128]{2,1,0:T(8,128)(2,1)S(1)}, u32[]{:S(2)}, u32[]{:S(2)}) %collective-permute-start.15) | collective-permute-done | bytes 36896 | tf_op jit(solution)/shard_map/ppermute | solution.py:250
  100.7 5.2 %shard_map.78 = (f32[2048,96]{1,0:T(8,128)}, bf16[2048,96]{1,0:T(8,128)(2,1)}, bf16[2048,96]{1,0:T(8,128)(2,1)}, bf16[2048,96]{1,0:T(8,128)(2,1)}, bf16[256,384]{1,0:T(8,128)(2,1)}) custom-call(s32[1]{0:T(128)} %bitcast.place, bf16[8,16,16,128]{3,2,1,0:T(8,128)(2,1)} %get-tuple-element.40.qa, f32[8,16,16,128]{3,2,1,0:T(8,128)} %get-tuple-element.41.dkv, ...), custom_call_target="tpu_custom_call" | custom-call | tf_op jit(solution)/shard_map/pallas_call | solution.py:307
  105.9 19.8 %all_to_all.10 = bf16[32,8,384]{2,1,0:T(8,128)(2,1)S(1)} all-to-all(bf16[32,8,384]{2,1,0:T(8,128)(2,1)} %bitcast.20), channel_id=1, replica_groups=mesh['gx'=8,'gy'=4,'ha'=4] {'gx','gy'}, dimensions={0} | all-to-all | bytes 393216 | tf_op jit(solution)/shard_map/all_to_all | solution.py:333
  126.4 4.2 %all-to-all-start.1 = ((bf16[32,8,384]{2,1,0:T(8,128)(2,1)}), bf16[32,8,384]{2,1,0:T(8,128)(2,1)S(1)}, u32[]{:S(2)}, u32[]{:S(2)}) async-start(bf16[32,8,384]{2,1,0:T(8,128)(2,1)} %broadcast_in_dim.2), calls=%async_computation.1 | async-start | bytes 393216 | tf_op jit(solution)/shard_map/all_to_all | solution.py:335
  130.6 1.6 %collective-permute-start.16 = (bf16[2048,96]{1,0:T(8,128)(2,1)}, bf16[2048,96]{1,0:T(8,128)(2,1)S(1)}, u32[]{:S(2)}, u32[]{:S(2)}) collective-permute-start(bf16[2048,96]{1,0:T(8,128)(2,1)} %get-tuple-element.51), channel_id=1, source_target_pairs={{0,1},{1,2},{2,3},{3,0},{4,5},{5,6},{6,7},{7,4},{8,9},{9,10},{10,1... | collective-permute-start | bytes 1179656 | tf_op jit(solution)/shard_map/ppermute | solution.py:328
  132.3 2.9 %collective-permute-start.17 = (bf16[2048,96]{1,0:T(8,128)(2,1)}, bf16[2048,96]{1,0:T(8,128)(2,1)S(1)}, u32[]{:S(2)}, u32[]{:S(2)}) collective-permute-start(bf16[2048,96]{1,0:T(8,128)(2,1)} %get-tuple-element.52), channel_id=1, source_target_pairs={{0,2},{1,3},{2,0},{3,1},{4,6},{5,7},{6,4},{7,5},{8,10},{9,11},{10,... | collective-permute-start | bytes 1179656 | tf_op jit(solution)/shard_map/ppermute | solution.py:328
  135.2 1.3 collective-permute-start.18
  136.5 2.1 %all-to-all-done.1 = bf16[32,8,384]{2,1,0:T(8,128)(2,1)S(1)} async-done(((bf16[32,8,384]{2,1,0:T(8,128)(2,1)}), bf16[32,8,384]{2,1,0:T(8,128)(2,1)S(1)}, u32[]{:S(2)}, u32[]{:S(2)}) %all-to-all-start.1) | async-done | bytes 196640 | tf_op jit(solution)/shard_map/all_to_all | solution.py:335
  140.1 6.2 %collective-permute-done.16 = bf16[2048,96]{1,0:T(8,128)(2,1)S(1)} collective-permute-done((bf16[2048,96]{1,0:T(8,128)(2,1)}, bf16[2048,96]{1,0:T(8,128)(2,1)S(1)}, u32[]{:S(2)}, u32[]{:S(2)}) %collective-permute-start.16) | collective-permute-done | bytes 393248 | tf_op jit(solution)/shard_map/ppermute | solution.py:328
  146.3 12.4 %collective-permute-done.17 = bf16[2048,96]{1,0:T(8,128)(2,1)S(1)} collective-permute-done((bf16[2048,96]{1,0:T(8,128)(2,1)}, bf16[2048,96]{1,0:T(8,128)(2,1)S(1)}, u32[]{:S(2)}, u32[]{:S(2)}) %collective-permute-start.17) | collective-permute-done | bytes 393248 | tf_op jit(solution)/shard_map/ppermute | solution.py:328
  (63 shorter events, 13.8 us)
Async XLA Ops:
  8.0 28.6 %collective-permute-start = (bf16[49,16,128]{2,1,0:T(8,128)(2,1)}, bf16[49,16,128]{2,1,0:T(8,128)(2,1)S(1)}, u32[]{:S(2)}, u32[]{:S(2)}) collective-permute-start(bf16[49,16,128]{2,1,0:T(8,128)(2,1)} %get-tuple-element.32), channel_id=1, source_target_pairs={{16,0},{20,4},{24,8},{28,12},{32,16},{36,20},{40,24},{44,28},{48,3... | collective-permute-start | bytes 602120 | tf_op jit(solution)/shard_map/ppermute | solution.py:250
  9.3 27.3 %collective-permute-start.1 = (bf16[49,16,128]{2,1,0:T(8,128)(2,1)}, bf16[49,16,128]{2,1,0:T(8,128)(2,1)S(1)}, u32[]{:S(2)}, u32[]{:S(2)}) collective-permute-start(bf16[49,16,128]{2,1,0:T(8,128)(2,1)} %get-tuple-element.33), channel_id=1, source_target_pairs={{0,16},{4,20},{8,24},{12,28},{16,32},{20,36},{24,40},{28,44},{32,4... | collective-permute-start | bytes 602120 | tf_op jit(solution)/shard_map/ppermute | solution.py:250
  13.8 6.6 %collective-permute-start.4 = (bf16[10,16,128]{2,1,0:T(8,128)(2,1)}, bf16[10,16,128]{2,1,0:T(8,128)(2,1)S(1)}, u32[]{:S(2)}, u32[]{:S(2)}) collective-permute-start(bf16[10,16,128]{2,1,0:T(8,128)(2,1)} %get-tuple-element.36), channel_id=1, source_target_pairs={{20,0},{24,4},{28,8},{36,16},{40,20},{44,24},{52,32},{56,36},{60,4... | collective-permute-start | bytes 122888 | tf_op jit(solution)/shard_map/ppermute | solution.py:250
  15.1 8.3 %collective-permute-start.5 = (bf16[10,16,128]{2,1,0:T(8,128)(2,1)}, bf16[10,16,128]{2,1,0:T(8,128)(2,1)S(1)}, u32[]{:S(2)}, u32[]{:S(2)}) collective-permute-start(bf16[10,16,128]{2,1,0:T(8,128)(2,1)} %get-tuple-element.37), channel_id=1, source_target_pairs={{16,4},{20,8},{24,12},{32,20},{36,24},{40,28},{48,36},{52,40},{56,... | collective-permute-start | bytes 122888 | tf_op jit(solution)/shard_map/ppermute | solution.py:250
  15.8 20.7 %collective-permute-start.2 = (bf16[25,16,128]{2,1,0:T(8,128)(2,1)}, bf16[25,16,128]{2,1,0:T(8,128)(2,1)S(1)}, u32[]{:S(2)}, u32[]{:S(2)}) collective-permute-start(bf16[25,16,128]{2,1,0:T(8,128)(2,1)} %get-tuple-element.34), channel_id=1, source_target_pairs={{4,0},{8,4},{12,8},{20,16},{24,20},{28,24},{36,32},{40,36},{44,40}... | collective-permute-start | bytes 307208 | tf_op jit(solution)/shard_map/ppermute | solution.py:250
  20.5 16.1 %copy-start.9 = (bf16[10,16,128]{2,1,0:T(8,128)(2,1)}, bf16[10,16,128]{2,1,0:T(8,128)(2,1)S(1)}, u32[]{:S(2)}) copy-start(bf16[10,16,128]{2,1,0:T(8,128)(2,1)S(1)} %collective-permute-done.4.refs_4_) | copy-start | bytes 122884
  20.5 16.1 %collective-permute-start.3 = (bf16[25,16,128]{2,1,0:T(8,128)(2,1)}, bf16[25,16,128]{2,1,0:T(8,128)(2,1)S(1)}, u32[]{:S(2)}, u32[]{:S(2)}) collective-permute-start(bf16[25,16,128]{2,1,0:T(8,128)(2,1)} %get-tuple-element.35), channel_id=1, source_target_pairs={{0,4},{4,8},{8,12},{16,20},{20,24},{24,28},{32,36},{36,40},{40,44}... | collective-permute-start | bytes 307208 | tf_op jit(solution)/shard_map/ppermute | solution.py:250
  23.4 0.7 collective-permute-start.6
  24.1 12.4 %collective-permute-start.7 = (bf16[10,16,128]{2,1,0:T(8,128)(2,1)}, bf16[10,16,128]{2,1,0:T(8,128)(2,1)S(1)}, u32[]{:S(2)}, u32[]{:S(2)}) collective-permute-start(bf16[10,16,128]{2,1,0:T(8,128)(2,1)} %get-tuple-element.39), channel_id=1, source_target_pairs={{0,20},{4,24},{8,28},{16,36},{20,40},{24,44},{32,52},{36,56},{40,6... | collective-permute-start | bytes 122888 | tf_op jit(solution)/shard_map/ppermute | solution.py:250
  67.2 32.6 %collective-permute-start.8 = (bf16[48,16,128]{2,1,0:T(8,128)(2,1)}, bf16[48,16,128]{2,1,0:T(8,128)(2,1)S(1)}, u32[]{:S(2)}, u32[]{:S(2)}) collective-permute-start(bf16[48,16,128]{2,1,0:T(8,128)(2,1)} %get-tuple-element.42), channel_id=1, source_target_pairs={{16,0},{20,4},{24,8},{28,12},{32,16},{36,20},{40,24},{44,28},{48,3... | collective-permute-start | bytes 589832 | tf_op jit(solution)/shard_map/ppermute | solution.py:250
  68.5 31.4 %collective-permute-start.9 = (bf16[48,16,128]{2,1,0:T(8,128)(2,1)}, bf16[48,16,128]{2,1,0:T(8,128)(2,1)S(1)}, u32[]{:S(2)}, u32[]{:S(2)}) collective-permute-start(bf16[48,16,128]{2,1,0:T(8,128)(2,1)} %get-tuple-element.43), channel_id=1, source_target_pairs={{0,16},{4,20},{8,24},{12,28},{16,32},{20,36},{24,40},{28,44},{32,4... | collective-permute-start | bytes 589832 | tf_op jit(solution)/shard_map/ppermute | solution.py:250
  77.3 7.8 %collective-permute-start.12 = (bf16[9,16,128]{2,1,0:T(8,128)(2,1)}, bf16[9,16,128]{2,1,0:T(8,128)(2,1)S(1)}, u32[]{:S(2)}, u32[]{:S(2)}) collective-permute-start(bf16[9,16,128]{2,1,0:T(8,128)(2,1)} %get-tuple-element.46), channel_id=1, source_target_pairs={{20,0},{24,4},{28,8},{36,16},{40,20},{44,24},{52,32},{56,36},{60,4... | collective-permute-start | bytes 110600 | tf_op jit(solution)/shard_map/ppermute | solution.py:250
  78.6 7.8 %collective-permute-start.13 = (bf16[9,16,128]{2,1,0:T(8,128)(2,1)}, bf16[9,16,128]{2,1,0:T(8,128)(2,1)S(1)}, u32[]{:S(2)}, u32[]{:S(2)}) collective-permute-start(bf16[9,16,128]{2,1,0:T(8,128)(2,1)} %get-tuple-element.47), channel_id=1, source_target_pairs={{16,4},{20,8},{24,12},{32,20},{36,24},{40,28},{48,36},{52,40},{56,... | collective-permute-start | bytes 110600 | tf_op jit(solution)/shard_map/ppermute | solution.py:250
  79.3 20.6 %collective-permute-start.10 = (bf16[24,16,128]{2,1,0:T(8,128)(2,1)}, bf16[24,16,128]{2,1,0:T(8,128)(2,1)S(1)}, u32[]{:S(2)}, u32[]{:S(2)}) collective-permute-start(bf16[24,16,128]{2,1,0:T(8,128)(2,1)} %get-tuple-element.44), channel_id=1, source_target_pairs={{4,0},{8,4},{12,8},{20,16},{24,20},{28,24},{36,32},{40,36},{44,40}... | collective-permute-start | bytes 294920 | tf_op jit(solution)/shard_map/ppermute | solution.py:250
  85.1 14.9 %copy-start.13 = (bf16[9,16,128]{2,1,0:T(8,128)(2,1)}, bf16[9,16,128]{2,1,0:T(8,128)(2,1)S(1)}, u32[]{:S(2)}) copy-start(bf16[9,16,128]{2,1,0:T(8,128)(2,1)S(1)} %collective-permute-done.12.refs_4_) | copy-start | bytes 110596
  85.1 14.8 %collective-permute-start.11 = (bf16[24,16,128]{2,1,0:T(8,128)(2,1)}, bf16[24,16,128]{2,1,0:T(8,128)(2,1)S(1)}, u32[]{:S(2)}, u32[]{:S(2)}) collective-permute-start(bf16[24,16,128]{2,1,0:T(8,128)(2,1)} %get-tuple-element.45), channel_id=1, source_target_pairs={{0,4},{4,8},{8,12},{16,20},{20,24},{24,28},{32,36},{36,40},{40,44}... | collective-permute-start | bytes 294920 | tf_op jit(solution)/shard_map/ppermute | solution.py:250
  86.4 13.6 %copy-start.14 = (bf16[9,16,128]{2,1,0:T(8,128)(2,1)}, bf16[9,16,128]{2,1,0:T(8,128)(2,1)S(1)}, u32[]{:S(2)}) copy-start(bf16[9,16,128]{2,1,0:T(8,128)(2,1)S(1)} %collective-permute-done.13.refs_5_) | copy-start | bytes 110596
  86.4 0.7 collective-permute-start.14
  87.1 12.8 %collective-permute-start.15 = (bf16[9,16,128]{2,1,0:T(8,128)(2,1)}, bf16[9,16,128]{2,1,0:T(8,128)(2,1)S(1)}, u32[]{:S(2)}, u32[]{:S(2)}) collective-permute-start(bf16[9,16,128]{2,1,0:T(8,128)(2,1)} %get-tuple-element.49), channel_id=1, source_target_pairs={{0,20},{4,24},{8,28},{16,36},{20,40},{24,44},{32,52},{36,56},{40,6... | collective-permute-start | bytes 110600 | tf_op jit(solution)/shard_map/ppermute | solution.py:250
  105.9 52.8 %copy-start = (f32[2048,96]{1,0:T(8,128)S(1)}, f32[2048,96]{1,0:T(8,128)}, u32[]{:S(2)}) copy-start(f32[2048,96]{1,0:T(8,128)} %get-tuple-element.50) | copy-start | bytes 2359300
  126.4 12.3 %all-to-all-start.1 = ((bf16[32,8,384]{2,1,0:T(8,128)(2,1)}), bf16[32,8,384]{2,1,0:T(8,128)(2,1)S(1)}, u32[]{:S(2)}, u32[]{:S(2)}) async-start(bf16[32,8,384]{2,1,0:T(8,128)(2,1)} %broadcast_in_dim.2), calls=%async_computation.1 | async-start | bytes 393216 | tf_op jit(solution)/shard_map/all_to_all | solution.py:335
  130.6 15.7 %collective-permute-start.16 = (bf16[2048,96]{1,0:T(8,128)(2,1)}, bf16[2048,96]{1,0:T(8,128)(2,1)S(1)}, u32[]{:S(2)}, u32[]{:S(2)}) collective-permute-start(bf16[2048,96]{1,0:T(8,128)(2,1)} %get-tuple-element.51), channel_id=1, source_target_pairs={{0,1},{1,2},{2,3},{3,0},{4,5},{5,6},{6,7},{7,4},{8,9},{9,10},{10,1... | collective-permute-start | bytes 1179656 | tf_op jit(solution)/shard_map/ppermute | solution.py:328
  132.3 26.4 %collective-permute-start.17 = (bf16[2048,96]{1,0:T(8,128)(2,1)}, bf16[2048,96]{1,0:T(8,128)(2,1)S(1)}, u32[]{:S(2)}, u32[]{:S(2)}) collective-permute-start(bf16[2048,96]{1,0:T(8,128)(2,1)} %get-tuple-element.52), channel_id=1, source_target_pairs={{0,2},{1,3},{2,0},{3,1},{4,6},{5,7},{6,4},{7,5},{8,10},{9,11},{10,... | collective-permute-start | bytes 1179656 | tf_op jit(solution)/shard_map/ppermute | solution.py:328
  135.2 23.5 %collective-permute-start.18 = (bf16[2048,96]{1,0:T(8,128)(2,1)}, bf16[2048,96]{1,0:T(8,128)(2,1)S(1)}, u32[]{:S(2)}, u32[]{:S(2)}) collective-permute-start(bf16[2048,96]{1,0:T(8,128)(2,1)} %get-tuple-element.53), channel_id=1, source_target_pairs={{0,3},{1,0},{2,1},{3,2},{4,7},{5,4},{6,5},{7,6},{8,11},{9,8},{10,9... | collective-permute-start | bytes 1179656 | tf_op jit(solution)/shard_map/ppermute | solution.py:328
  (13 other events, 45.4 us)

commit v2 on v1

v2 whole, which is shorter than its diff:
```python
import jax
import jax.numpy as jnp
from jax import lax
from jax.experimental import pallas as pl
from jax.experimental.pallas import tpu as pltpu
from jax.sharding import PartitionSpec as P


HD = 64
REACH = 3
LANES = 128
BLOCK = 4
SPAN = BLOCK + 2 * REACH
BIG = 2.0**100
F32 = jnp.float32
BF16 = jnp.bfloat16
LANE_X = 64
LANE_Y = 72
LANE_Z = 88
LANE_F = 104

STEPS = (-1, 1)


def dot(a, b):
    return lax.dot_general(a, b, (((1,), (0,)), ((), ())), preferred_element_type=F32)


def dot_t(a, b):
    return lax.dot_general(a, b, (((1,), (1,)), ((), ())), preferred_element_type=F32)


def edge(step, extent):
    if step < 0:
        return 0, REACH
    if step > 0:
        return extent - REACH, extent
    return 0, extent


def halo(step, extent):
    if step < 0:
        return 0, REACH
    if step > 0:
        return extent + REACH, extent + 2 * REACH
    return REACH, extent + REACH


def project_kernel(tok, cot, w, wo, bits, kv_o, qu_o, *sends):
    nx, ny, nz, _ = kv_o.shape
    weight = w[...]
    wide = jnp.concatenate(
        [weight[HD:], weight[:HD], jnp.zeros((HD, weight.shape[1]), BF16)], axis=0
    )
    out_w = jnp.concatenate([jnp.zeros((HD, weight.shape[1]), BF16), wo[...]], axis=0)
    z = lax.broadcasted_iota(jnp.int32, (nz, LANES), 0)
    flags = (lax.shift_right_logical(jnp.broadcast_to(bits[...], (nz, LANES)), z) & 1).astype(F32)
    flags = flags.astype(BF16)
    rows = ny * nz
    for x in range(nx):
        part = dot_t(tok[x * rows : (x + 1) * rows, :], wide)
        ups = dot_t(cot[x * rows : (x + 1) * rows, :], out_w)
        kv_o[x] = part[:, :LANES].astype(BF16).reshape(ny, nz, LANES)
        qu_o[x] = (part[:, LANES:] + ups).astype(BF16).reshape(ny, nz, LANES)
    for step, out in zip(STEPS, sends[:2]):
        y0, y1 = edge(step, ny)
        for x in range(nx):
            out[x * REACH : (x + 1) * REACH] = kv_o[x, y0:y1]
        out[nx * REACH] = flags
    sends[2][...] = flags


def pack_kernel(kv, flags, low, high, kvc_o, tags_o, *sends):
    nx, ny, _, _ = kv.shape
    wy = ny + 2 * REACH
    for x in range(nx):
        kvc_o[x, REACH : REACH + ny] = kv[x]
        kvc_o[x, :REACH] = low[x * REACH : (x + 1) * REACH]
        kvc_o[x, REACH + ny :] = high[x * REACH : (x + 1) * REACH]
    tiles = (low[nx * REACH], flags[...], high[nx * REACH])
    for t, tile in enumerate(tiles):
        tags_o[t] = tile
    for step, out in zip(STEPS, sends):
        x0, x1 = edge(step, nx)
        for x in range(x0, x1):
            out[(x - x0) * wy : (x - x0 + 1) * wy] = kvc_o[x]
        for t, tile in enumerate(tiles):
            out[REACH * wy + t] = tile


class Bias:
    def __init__(self, nx, ny, nz):
        self.nx, self.ny, self.nz = nx, ny, nz
        self.lane = lax.broadcasted_iota(jnp.int32, (nz, LANES), 1)
        zrow = lax.broadcasted_iota(jnp.int32, (nz, LANES), 0)
        far = self.mine(LANE_Z, nz) & (jnp.abs(self.lane - LANE_Z - zrow) > REACH)
        base_z = jnp.where(far, -BIG, 0.0).astype(F32)
        self.base_y = [self.base(LANE_Y, ny, y) + base_z for y in range(ny + 2 * REACH)]

    def mine(self, first, extent):
        return (self.lane >= first) & (self.lane < first + extent)

    def base(self, first, extent, at):
        far = jnp.abs(self.lane - first - (at - REACH)) > REACH
        return jnp.where(self.mine(first, extent) & far, -BIG, 0.0)

    def rolled(self, tile, x):
        shift = (LANE_F - x * self.ny) % LANES
        value = (tile.astype(F32) - 1.0) * BIG
        return pltpu.roll(value, shift, 1) if shift else value

    def fill(self, source, tiles, kx, x, target):
        base_x = self.base(LANE_X, self.nx, kx)
        planes = [self.rolled(tile, x) for tile in tiles]
        for y in range(self.ny + 2 * REACH):
            which = 0 if y < REACH else 1 if y < REACH + self.ny else 2
            at = (y - REACH) % self.ny
            flag = jnp.where(self.lane == LANE_F + at, planes[which], 0.0)
            bias = (base_x + self.base_y[y] + flag).astype(BF16)
            target(y, jnp.where(self.lane < HD, source(y), bias))


def block_of(index, ny):
    blocks_y = ny // BLOCK
    half = index // blocks_y
    return half, half * BLOCK, index % blocks_y * BLOCK


def near_planes(half, x0):
    own = [x0 + i for i in range(BLOCK)]
    return own + [BLOCK - REACH * half + i for i in range(REACH)]


def local_kernel(kvc, qu, tags, e_o, stat_o, aug_o, up_o, kaug):
    nx, wy, nz, _ = kvc.shape
    ny = wy - 2 * REACH
    bias = Bias(nx, ny, nz)
    tiles = [tags[t] for t in range(3)]
    for x in range(nx):

        def target(y, value, x=x):
            kaug[x, y] = value

        bias.fill(lambda y, x=x: kvc[x, y], tiles, x + REACH, x, target)
    rows = BLOCK * BLOCK * nz
    keys = SPAN * nz
    strip = BLOCK * nz
    qlane = lax.broadcasted_iota(jnp.int32, (rows, LANES), 1)
    qrow = lax.broadcasted_iota(jnp.int32, (rows, LANES), 0)
    drow = lax.broadcasted_iota(jnp.int32, (strip, rows), 0)
    dlane = lax.broadcasted_iota(jnp.int32, (strip, rows), 1)
    scale = HD ** (-0.5)

    def one(index, carry):
        half, x0, y0 = block_of(index, ny)
        both = qu[pl.ds(x0, BLOCK), pl.ds(y0, BLOCK)].reshape(rows, LANES)
        qx = x0 + qrow // strip
        qy = y0 + qrow // nz % BLOCK
        hot = (
            (qlane == LANE_X + qx)
            | (qlane == LANE_Y + qy)
            | (qlane == LANE_Z + qrow % nz)
            | ((qlane >= LANE_F) & (qlane < LANE_F + ny))
        )
        wide = both.astype(F32)
        qlow = qlane < HD
        scaled = jnp.where(qlow, wide * scale, 0.0)
        aug = jnp.where(qlow, scaled, jnp.where(hot, 1.0, 0.0))
        aug_t = aug.T.astype(BF16)
        q_t = scaled.T.astype(BF16)
        aug_o[index] = aug_t
        up_o[index] = jnp.where(qlow, 0.0, wide).T.astype(BF16)
        top = jnp.full((8, rows), -jnp.inf, F32)
        planes = near_planes(half, x0)
        for j, x in enumerate(planes):
            s = dot(kaug[x, pl.ds(y0, SPAN)].reshape(keys, LANES), aug_t)
            if j < BLOCK:
                mid = kvc[x, pl.ds(y0 + REACH, BLOCK)].reshape(strip, LANES)
                plain = dot(mid, q_t)
                diagonal = dlane - j * strip == drow
                a, b = REACH * nz, REACH * nz + strip
                s = jnp.concatenate([s[:a], jnp.where(diagonal, plain, s[a:b]), s[b:]], axis=0)
            e_o[index, j] = s
            top = jnp.maximum(top, jnp.max(s.reshape(keys // 8, 8, rows), axis=0))
        top = jnp.max(top, axis=0, keepdims=True)
        total = jnp.zeros((8, rows), F32)
        for j in range(len(planes)):
            e = jnp.exp(e_o[index, j] - top)
            e_o[index, j] = e
            total = total + jnp.sum(e.reshape(keys // 8, 8, rows), axis=0)
        stat_o[index, 0] = jnp.broadcast_to(top, (8, rows))
        stat_o[index, 1] = total
        return carry

    lax.fori_loop(0, (nx // BLOCK) * (ny // BLOCK), one, 0)


def mixed_of(qu, x0, y0):
    nz = qu.shape[2]
    rows = BLOCK * BLOCK * nz
    wide = qu[pl.ds(x0, BLOCK), pl.ds(y0, BLOCK)].reshape(rows, LANES).astype(F32)
    qlow = lax.broadcasted_iota(jnp.int32, (rows, LANES), 1) < HD
    scaled = jnp.where(qlow, wide * HD ** (-0.5), 0.0)
    return jnp.concatenate([scaled, jnp.where(qlow, 0.0, wide)], axis=0).astype(BF16)


def far_kernel(kvc, qu, e_i, stat, aug, up, low, high, *refs):
    p_o, r_o, dqo_o = refs[:3]
    backs = refs[3:5]
    kvh, kaug, acc, s_scr, d_scr = refs[5:]
    nx, wy, nz, _ = kvc.shape
    ny = wy - 2 * REACH
    bias = Bias(nx, ny, nz)
    for side, piece in enumerate((low, high)):
        tiles = [piece[REACH * wy + t] for t in range(3)]
        first = halo(STEPS[side], nx)[0]
        own = edge(-STEPS[side], nx)[0]
        for i in range(REACH):
            kvh[side, i] = piece[i * wy : (i + 1) * wy]

            def target(y, value, side=side, i=i):
                kaug[side, i, y] = value

            bias.fill(
                lambda y, i=i, piece=piece: piece[i * wy + y], tiles, first + i, own + i, target
            )
    acc[...] = jnp.zeros(acc.shape, F32)
    rows = BLOCK * BLOCK * nz
    keys = SPAN * nz
    scale = HD ** (-0.5)
    near = BLOCK + REACH

    def one(index, carry):
        half, x0, y0 = block_of(index, ny)
        aug_t = aug[index]
        u_t = up[index]
        mixed = mixed_of(qu, x0, y0)
        before = stat[index, 0, :1]
        top = jnp.full((8, rows), -jnp.inf, F32)
        for i in range(REACH):
            s = dot(kaug[half, i, pl.ds(y0, SPAN)].reshape(keys, LANES), aug_t)
            s_scr[i] = s
            top = jnp.maximum(top, jnp.max(s.reshape(keys // 8, 8, rows), axis=0))
        top = jnp.maximum(jnp.max(top, axis=0, keepdims=True), before)
        shrink = jnp.exp(before - top)
        total = stat[index, 1] * shrink
        for i in range(REACH):
            e = jnp.exp(s_scr[i] - top)
            s_scr[i] = e
            total = total + jnp.sum(e.reshape(keys // 8, 8, rows), axis=0)
        inverse = 1.0 / jnp.sum(total, axis=0, keepdims=True)
        shrunk = shrink * inverse
        for j in range(near):
            p_o[index, j * keys : (j + 1) * keys] = (e_i[index, j] * shrunk).astype(BF16)
        for i in range(REACH):
            j = near + i
            p_o[index, j * keys : (j + 1) * keys] = (s_scr[i] * inverse).astype(BF16)
        planes = near_planes(half, x0)
        block = [kvc[x, pl.ds(y0, SPAN)].reshape(keys, LANES) for x in planes]
        outer = [kvh[half, i, pl.ds(y0, SPAN)].reshape(keys, LANES) for i in range(REACH)]
        block_t = jnp.concatenate(block + outer, axis=0).T
        o_t = dot(block_t[HD:], p_o[index])
        r = jnp.sum(u_t[HD:].astype(F32) * o_t, axis=0, keepdims=True)
        r_o[index] = jnp.broadcast_to(r, (8, rows))
        for i in range(REACH):
            j = near + i
            g = dot(outer[i], u_t)
            p = p_o[index, j * keys : (j + 1) * keys]
            ds = (p.astype(F32) * (g - r)).astype(BF16)
            d_scr[i * keys : (i + 1) * keys] = ds
            grad = dot(jnp.concatenate([ds, p], axis=1), mixed)
            acc[half, i, pl.ds(y0, SPAN)] += grad.reshape(SPAN, nz, LANES)
        dqo_o[index, :HD] = dot(block_t[:HD, near * keys :], d_scr[...]) * scale
        dqo_o[index, HD:] = o_t
        return carry

    lax.fori_loop(0, (nx // BLOCK) * (ny // BLOCK), one, 0)
    for side, out in enumerate(backs):
        for i in range(REACH):
            out[i * wy : (i + 1) * wy] = acc[side, i].astype(BF16)


def near_kernel(kvc, qu, p_i, r_i, up, dqo, qa_o, dkv_o, d_scr):
    nx, wy, nz, _ = kvc.shape
    ny = wy - 2 * REACH
    keys = SPAN * nz
    scale = HD ** (-0.5)
    dkv_o[...] = jnp.zeros(dkv_o.shape, F32)

    def one(index, carry):
        half, x0, y0 = block_of(index, ny)
        u_t = up[index]
        mixed = mixed_of(qu, x0, y0)
        r = r_i[index, :1]
        planes = near_planes(half, x0)
        block = [kvc[x, pl.ds(y0, SPAN)].reshape(keys, LANES) for x in planes]
        for j, x in enumerate(planes):
            g = dot(block[j], u_t)
            p = p_i[index, j * keys : (j + 1) * keys]
            ds = (p.astype(F32) * (g - r)).astype(BF16)
            d_scr[j * keys : (j + 1) * keys] = ds
            grad = dot(jnp.concatenate([ds, p], axis=1), mixed)
            dkv_o[x, pl.ds(y0, SPAN)] += grad.reshape(SPAN, nz, LANES)
        block_t = jnp.concatenate(block, axis=0).T
        q_grad = dot(block_t[:HD], d_scr[...]) * scale + dqo[index, :HD]
        result = jnp.concatenate([q_grad, dqo[index, HD:]], axis=0).T
        qa_o[pl.ds(x0, BLOCK), pl.ds(y0, BLOCK)] = result.astype(BF16).reshape(
            BLOCK, BLOCK, nz, LANES
        )
        return carry

    lax.fori_loop(0, (nx // BLOCK) * (ny // BLOCK), one, 0)


def returned(dkv, pieces, x, y0, y1):
    nx, wy = dkv.shape[:2]
    value = dkv[x, y0:y1]
    for step, piece in zip(STEPS, pieces):
        a, b = edge(step, nx)
        if a <= x < b:
            value = value + piece[(x - a) * wy + y0 : (x - a) * wy + y1].astype(F32)
    return value


def rim_kernel(dkv, low, high, *sends):
    nx, wy = dkv.shape[:2]
    ny = wy - 2 * REACH
    for step, out in zip(STEPS, sends):
        y0, y1 = halo(step, ny)
        for x in range(nx):
            rim = returned(dkv, (low, high), x, y0, y1)
            out[x * REACH : (x + 1) * REACH] = rim.astype(BF16)


def tail_kernel(place, qa, dkv, low, high, tok, cot, w, south, north, *refs):
    own_o, sends, sums_o, grads = refs[0], refs[1:-2], refs[-2], refs[-1]
    nx, ny, nz, _ = qa.shape
    rows = nx * ny * nz
    plane = ny * nz
    for x in range(nx):
        value = returned(dkv, (low, high), x, REACH, REACH + ny)
        parts = []
        for step, piece in zip(STEPS, (south, north)):
            a, b = edge(step, ny)
            parts.append(value[a:b] + piece[x * REACH : (x + 1) * REACH].astype(F32))
        value = jnp.concatenate([parts[0], value[REACH : ny - REACH], parts[1]], axis=0)
        grads[x * plane : (x + 1) * plane, :LANES] = value.reshape(plane, LANES).astype(BF16)
    grads[:, LANES:] = qa[...].reshape(rows, LANES)
    count = w.shape[0]
    mine = place[0]

    def share(step):
        chunk = w[lax.rem(mine + step, count)]
        wide = jnp.concatenate(
            [chunk[:, HD:], chunk[:, :HD], jnp.zeros((chunk.shape[0], HD), BF16)], axis=1
        )
        return dot_t(grads[...], wide)

    for step in range(1, count):
        sends[step - 1][...] = share(step).astype(BF16)
    own_o[...] = share(0)
    grads_t = grads[...].T
    sums_o[: 3 * HD] = dot(grads_t[: 3 * HD], tok[...]).astype(BF16)
    sums_o[3 * HD :] = dot(grads_t[3 * HD :], cot[...]).astype(BF16)


def shifted(pieces, axis):
    count = lax.axis_size(axis)
    up = [(i, i + 1) for i in range(count - 1)]
    down = [(target, source) for source, target in up]
    to_low, to_high = pieces
    from_low = lax.ppermute(to_high, axis, up)
    from_high = lax.ppermute(to_low, axis, down)
    return from_low, from_high


def call(kernel, outs, scratch=(), scalars=0, count=0, limit=20):
    vmem = pl.BlockSpec(memory_space=pltpu.VMEM)
    smem = pl.BlockSpec(memory_space=pltpu.SMEM)
    return pl.pallas_call(
        kernel,
        out_shape=outs,
        in_specs=[smem] * scalars + [vmem] * (count - scalars),
        out_specs=[vmem] * len(outs),
        scratch_shapes=list(scratch),
        compiler_params=pltpu.CompilerParams(vmem_limit_bytes=limit << 20),
    )


def shards(tokens, input_weight, output_weight, tissue_bits, cotangent):
    nx, ny, nz, model = tokens.shape
    rows = nx * ny * nz
    wy = ny + 2 * REACH
    flat_tokens = tokens.reshape(rows, model)
    flat_cotangent = cotangent.reshape(rows, model)
    blocks = (nx // BLOCK) * (ny // BLOCK)
    keys = SPAN * nz
    queries = BLOCK * BLOCK * nz
    near = BLOCK + REACH

    def half(*dims):
        return jax.ShapeDtypeStruct(dims, BF16)

    def full(*dims):
        return jax.ShapeDtypeStruct(dims, F32)

    grid = half(nx, ny, nz, LANES)
    rim_y = REACH * nx
    rim_x = REACH * wy
    kv, qu, y_low, y_high, flags = call(
        project_kernel,
        [grid, grid] + [half(rim_y + 1, nz, LANES)] * 2 + [half(nz, LANES)],
        count=5,
    )(
        flat_tokens,
        flat_cotangent,
        input_weight.T,
        output_weight,
        tissue_bits.reshape(1, nx * ny),
    )
    south, north = shifted((y_low, y_high), "gy")
    kvc, tags, x_low, x_high = call(
        pack_kernel,
        [half(nx, wy, nz, LANES), half(3, nz, LANES)] + [half(rim_x + 3, nz, LANES)] * 2,
        count=4,
    )(kv, flags, south, north)
    west, east = shifted((x_low, x_high), "gx")
    e, stat, aug, up = call(
        local_kernel,
        [
            full(blocks, near, keys, queries),
            full(blocks, 2, 8, queries),
            half(blocks, LANES, queries),
            half(blocks, LANES, queries),
        ],
        scratch=[pltpu.VMEM((nx, wy, nz, LANES), BF16)],
        count=3,
    )(kvc, qu, tags)
    p, r, dqo, back_low, back_high = call(
        far_kernel,
        [
            half(blocks, SPAN * keys, queries),
            full(blocks, 8, queries),
            full(blocks, LANES, queries),
        ]
        + [half(rim_x, nz, LANES)] * 2,
        scratch=[
            pltpu.VMEM((2, REACH, wy, nz, LANES), BF16),
            pltpu.VMEM((2, REACH, wy, nz, LANES), BF16),
            pltpu.VMEM((2, REACH, wy, nz, LANES), F32),
            pltpu.VMEM((REACH, keys, queries), F32),
            pltpu.VMEM((REACH * keys, queries), BF16),
        ],
        count=8,
    )(kvc, qu, e, stat, aug, up, west, east)
    low, high = shifted((back_low, back_high), "gx")
    qa, dkv = call(
        near_kernel,
        [grid, full(nx, wy, nz, LANES)],
        scratch=[pltpu.VMEM((near * keys, queries), BF16)],
        count=6,
    )(kvc, qu, p, r, up, dqo)
    rims = call(rim_kernel, [half(rim_y, nz, LANES)] * 2, count=3)(dkv, low, high)
    south, north = shifted(rims, "gy")
    parts = lax.axis_size("ha")
    width = model // parts
    mine = lax.axis_index("ha").astype(jnp.int32).reshape(1)
    own, *rest = call(
        tail_kernel,
        [full(rows, width)]
        + [half(rows, width)] * (parts - 1)
        + [half(4 * HD, model)],
        scratch=[pltpu.VMEM((rows, 2 * LANES), BF16)],
        scalars=1,
        count=10,
    )(
        mine,
        qa,
        dkv,
        low,
        high,
        flat_tokens,
        flat_cotangent,
        input_weight.reshape(parts, width, 3 * HD),
        south,
        north,
    )
    shares, sums = rest[:-1], rest[-1]
    total = own
    for step, piece in zip(range(1, parts), shares):
        ring = [(i, (i + step) % parts) for i in range(parts)]
        total = total + lax.ppermute(piece, "ha", ring).astype(F32)
    token_gradient = total.astype(BF16).reshape(nx, ny, nz, width)
    both = ("gx", "gy")
    members = lax.axis_size("gx") * lax.axis_size("gy")
    split = sums.reshape(members, 4 * HD // members, model)
    met = lax.all_to_all(split, both, 0, 0, tiled=True)
    mean = jnp.sum(met.astype(F32), axis=0, keepdims=True).astype(BF16)
    spread = lax.all_to_all(jnp.broadcast_to(mean, split.shape), both, 0, 0, tiled=True)
    normaliser = (rows * members) ** (-0.5)
    whole = spread.reshape(4 * HD, model).astype(F32) * normaliser
    input_gradient = jnp.concatenate([whole[2 * HD : 3 * HD], whole[: 2 * HD]], axis=0).T
    return token_gradient, input_gradient, whole[3 * HD :]


def solution(mesh):
    placed = (
        P("gx", "gy", None, None),
        P(None, "ha"),
        P("ha", None),
        P("gx", "gy"),
        P("gx", "gy", None, None),
    )

    return jax.shard_map(
        shards,
        mesh=mesh,
        in_specs=placed,
        out_specs=(P("gx", "gy", None, "ha"), P(None, "ha"), P("ha", None)),
        check_vma=False,
    )
```

time: 161 us -> 135 us (0.84)
  starting transfers between devices: 59.3 us -> 28 us
  local copies, waits for them, and re-layouts: 5.83 us -> 17.2 us
  Pallas kernels: 39.5 us -> 33.8 us
    ppermute x16 -> x8, starting transfers between devices: 49.2 us -> 18.5 us  [the longest x4 13.4 us: shifted(): from_low = lax.ppermute(to_high, axis, up)]
    unnamed x35 -> x37, local copies, waits for them, and re-layouts: 3.22 us -> 15.1 us
    pallas_call x3 -> x7, Pallas kernels: 39.5 us -> 33.8 us  [the longest x1 11.8 us: shards(): call(near_kernel, [grid, full(nx, wy, nz, LANES)], scratch=[pltpu.VMEM((n...]
    ppermute x16 -> x8, waiting for transfers between devices: 11.8 us -> 10.7 us  [the longest x4 10.7 us: shifted(): from_high = lax.ppermute(to_low, axis, down)]
  transfers between devices with their start and end apart: 20 -> 12, of which waited for: 7 -> 6; matrix products, arithmetic and copies ran while one was open for 1% -> 2% of each run, Pallas kernels for 0% -> 13%
where the time goes in v2:
time: 135 us; the launch traced here: 134 us
  Pallas kernels  33.8 us (25%)
  waiting for transfers between devices  33.6 us (25%)
  starting transfers between devices  28 us (21%)
  blocking collectives  19 us (14%)
  local copies, waits for them, and re-layouts  17.2 us (13%)
  other arithmetic  1.84 us (1%)
    ppermute x3, waiting for transfers between devices, shards(): total = total + lax.ppermute(piece, 'ha', ring).astype(F32)  20.1 us
    all_to_all x1, blocking collectives, shards(): met = lax.all_to_all(split, both, 0, 0, tiled=True)  19 us
    unnamed x37, local copies, waits for them, and re-layouts  15.1 us
    ppermute x4, starting transfers between devices, shifted(): from_low = lax.ppermute(to_high, axis, up)  13.4 us
    pallas_call x1, Pallas kernels, shards(): call(near_kernel, [grid, full(nx, wy, nz, LANES)], scratch=[pltpu.VMEM((n...  11.8 us
    pallas_call x1, Pallas kernels, shards(): call(far_kernel, [half(blocks, SPAN * keys, queries), full(blocks, 8, que...  11.4 us
    ppermute x4, waiting for transfers between devices, shifted(): from_high = lax.ppermute(to_low, axis, down)  10.7 us
    pallas_call x1, Pallas kernels, shards(): call(local_kernel, [full(blocks, near, keys, queries), full(blocks, 2, 8,...  5.63 us
  transfers between devices with their start and end apart: 12, of which 6 were waited for; matrix products, arithmetic and copies ran while one was open for 2% of the time, Pallas kernels for 13%

profile of v2, /device:TPU:0, one launch (start us, length us, event | category | flops | bytes accessed | tf_op | source)
XLA Modules:
  0.0 134.3 jit_solution(4582616277994047291)
XLA Ops:
  1.4 1.4 %copy-done = bf16[8,16,16,384]{3,2,1,0:T(8,128)(2,1)S(1)} copy-done((bf16[8,16,16,384]{3,2,1,0:T(8,128)(2,1)S(1)}, bf16[8,16,16,384]{3,2,1,0:T(8,128)(2,1)}, u32[]{:S(2)}) %copy-start) | copy-done | bytes 1572888
  2.8 1.4 %copy-done.2 = bf16[8,16,16,384]{3,2,1,0:T(8,128)(2,1)S(1)} copy-done((bf16[8,16,16,384]{3,2,1,0:T(8,128)(2,1)S(1)}, bf16[8,16,16,384]{3,2,1,0:T(8,128)(2,1)}, u32[]{:S(2)}) %copy-start.2) | copy-done | bytes 1572888
  7.2 1.3 collective-permute-start
  8.5 1.3 collective-permute-start.1
  9.8 5.3 %collective-permute-done.1.high = bf16[25,16,128]{2,1,0:T(8,128)(2,1)S(1)} collective-permute-done((bf16[25,16,128]{2,1,0:T(8,128)(2,1)S(1)}, bf16[25,16,128]{2,1,0:T(8,128)(2,1)S(1)}, u32[]{:S(2)}, u32[]{:S(2)}) %collective-permute-start.1) | collective-permute-done | bytes 102432 | tf_op jit(solution)/shard_map/ppermute | solution.py:373
  15.1 2.5 %collective-permute-start.2 = (bf16[69,16,128]{2,1,0:T(8,128)(2,1)S(1)}, bf16[69,16,128]{2,1,0:T(8,128)(2,1)S(1)}, u32[]{:S(2)}, u32[]{:S(2)}) collective-permute-start(bf16[69,16,128]{2,1,0:T(8,128)(2,1)S(1)} %get-tuple-element.41), channel_id=1, source_target_pairs={{0,16},{16,32},{32,48},{48,64},{64,80},{80,96},{96,112},{1,17},{17... | collective-permute-start | bytes 847880 | tf_op jit(solution)/shard_map/ppermute | solution.py:372
  17.7 1.3 collective-permute-start.3
  19.0 5.6 %shard_map.78 = (f32[8,7,160,256]{3,2,1,0:T(8,128)S(1)}, f32[8,2,8,256]{3,2,1,0:T(8,128)S(1)}, bf16[8,128,256]{2,1,0:T(8,128)(2,1)S(1)}, bf16[8,128,256]{2,1,0:T(8,128)(2,1)S(1)}) custom-call(bf16[8,22,16,128]{3,2,1,0:T(8,128)(2,1)S(1)} %get-tuple-element.34.kvc, bf16[8,16,16,128]{3,2,1,0:T(8,128)(2,1)S(1)} %get-tuple-element.35.qu, ...), custom_call_target="tpu_custom_call" | custom-call | tf_op jit(solution)/shard_map/pallas_call | solution.py:428
  24.6 5.0 %collective-permute-done.3.high = bf16[69,16,128]{2,1,0:T(8,128)(2,1)S(1)} collective-permute-done((bf16[69,16,128]{2,1,0:T(8,128)(2,1)S(1)}, bf16[69,16,128]{2,1,0:T(8,128)(2,1)S(1)}, u32[]{:S(2)}, u32[]{:S(2)}) %collective-permute-start.3) | collective-permute-done | bytes 282656 | tf_op jit(solution)/shard_map/ppermute | solution.py:373
  29.6 11.4 %shard_map.79 = (bf16[8,1600,256]{2,1,0:T(8,128)(2,1)S(1)}, f32[8,8,256]{2,1,0:T(8,128)S(1)}, f32[8,128,256]{2,1,0:T(8,128)S(1)}, bf16[66,16,128]{2,1,0:T(8,128)(2,1)S(1)}, bf16[66,16,128]{2,1,0:T(8,128)(2,1)S(1)}) custom-call(bf16[8,22,16,128]{3,2,1,0:T(8,128)(2,1)S(1)} %get-tuple-element.34.kvc, bf16[8,16,16,128]{3,2,1,0:T(8,128)(2,1)S(1)} %get-tuple-element.35.qu, ...), custom_call_target="tpu_custom_call" | custom-call | tf_op jit(solution)/shard_map/pallas_call | solution.py:439
  41.0 5.2 %collective-permute-start.4 = (bf16[66,16,128]{2,1,0:T(8,128)(2,1)S(1)}, bf16[66,16,128]{2,1,0:T(8,128)(2,1)S(1)}, u32[]{:S(2)}, u32[]{:S(2)}) collective-permute-start(bf16[66,16,128]{2,1,0:T(8,128)(2,1)S(1)} %get-tuple-element.48), channel_id=1, source_target_pairs={{0,16},{16,32},{32,48},{48,64},{64,80},{80,96},{96,112},{1,17},{17... | collective-permute-start | bytes 811016 | tf_op jit(solution)/shard_map/ppermute | solution.py:372
  47.5 11.8 %shard_map.80 = (bf16[8,16,16,128]{3,2,1,0:T(8,128)(2,1)S(1)}, f32[8,22,16,128]{3,2,1,0:T(8,128)S(1)}) custom-call(bf16[8,22,16,128]{3,2,1,0:T(8,128)(2,1)S(1)} %get-tuple-element.34.kvc, bf16[8,16,16,128]{3,2,1,0:T(8,128)(2,1)S(1)} %get-tuple-element.35.qu, bf16[8,1600,256]{2,1,0:T(8,128)(2,1)S(1)} %get-tuple-element.43.p_i, ...), custom_call_target="tpu_custom_call" | custom-call | tf_op jit(solution)/shard_map/pallas_call | solution.py:457
  61.3 4.4 %collective-permute-start.6 = (bf16[24,16,128]{2,1,0:T(8,128)(2,1)}, bf16[24,16,128]{2,1,0:T(8,128)(2,1)S(1)}, u32[]{:S(2)}, u32[]{:S(2)}) collective-permute-start(bf16[24,16,128]{2,1,0:T(8,128)(2,1)} %get-tuple-element.50), channel_id=1, source_target_pairs={{0,4},{4,8},{8,12},{1,5},{5,9},{9,13},{2,6},{6,10},{10,14},{3,7},{... | collective-permute-start | bytes 294920 | tf_op jit(solution)/shard_map/ppermute | solution.py:372
  65.7 1.3 collective-permute-start.7
  67.0 1.7 %copy.8 = bf16[384,192]{1,0:T(8,128)(2,1)} copy(bf16[384,192]{0,1:T(8,128)(2,1)} %param.6) | data formatting | bytes 294912 | tf_op args[1]
  69.2 1.4 %copy-done.5 = f32[8,22,16,128]{3,2,1,0:T(8,128)S(1)} copy-done((f32[8,22,16,128]{3,2,1,0:T(8,128)S(1)}, f32[8,22,16,128]{3,2,1,0:T(8,128)}, u32[]{:S(2)}) %copy-start.5) | copy-done | bytes 1441816
  73.5 2.9 %shard_map.82 = (f32[2048,96]{1,0:T(8,128)S(1)}, bf16[2048,96]{1,0:T(8,128)(2,1)S(1)}, bf16[2048,96]{1,0:T(8,128)(2,1)S(1)}, bf16[2048,96]{1,0:T(8,128)(2,1)S(1)}, bf16[256,384]{1,0:T(8,128)(2,1)S(1)}) custom-call(s32[1]{0:T(128)} %bitcast.place, bf16[8,16,16,128]{3,2,1,0:T(8,128)(2,1)S(1)} %copy-done.13, f32[8,22,16,128]{3,2,1,0:T(8,128)S(1)} %copy-done.5, ...), custom_call_target="tpu_custom_call" | custom-call | tf_op jit(solution)/shard_map/pallas_call | solution.py:468
  79.7 19.0 %all_to_all.10 = bf16[32,8,384]{2,1,0:T(8,128)(2,1)S(1)} all-to-all(bf16[32,8,384]{2,1,0:T(8,128)(2,1)S(1)} %bitcast.21), channel_id=1, replica_groups=mesh['gx'=8,'gy'=4,'ha'=4] {'gx','gy'}, dimensions={0} | all-to-all | bytes 393216 | tf_op jit(solution)/shard_map/all_to_all | solution.py:497
  99.4 4.2 %all-to-all-start.1 = ((bf16[32,8,384]{2,1,0:T(8,128)(2,1)}), bf16[32,8,384]{2,1,0:T(8,128)(2,1)S(1)}, u32[]{:S(2)}, u32[]{:S(2)}) async-start(bf16[32,8,384]{2,1,0:T(8,128)(2,1)} %broadcast_in_dim.2), calls=%async_computation.1 | async-start | bytes 393216 | tf_op jit(solution)/shard_map/all_to_all | solution.py:499
  103.7 3.1 %collective-permute-start.10 = (bf16[2048,96]{1,0:T(8,128)(2,1)}, bf16[2048,96]{1,0:T(8,128)(2,1)S(1)}, u32[]{:S(2)}, u32[]{:S(2)}) collective-permute-start(bf16[2048,96]{1,0:T(8,128)(2,1)} %copy-done.17), channel_id=1, source_target_pairs={{0,3},{1,0},{2,1},{3,2},{4,7},{5,4},{6,5},{7,6},{8,11},{9,8},{10,9... | collective-permute-start | bytes 1179656 | tf_op jit(solution)/shard_map/ppermute | solution.py:492
  106.8 2.2 %collective-permute-start.9 = (bf16[2048,96]{1,0:T(8,128)(2,1)}, bf16[2048,96]{1,0:T(8,128)(2,1)S(1)}, u32[]{:S(2)}, u32[]{:S(2)}) collective-permute-start(bf16[2048,96]{1,0:T(8,128)(2,1)} %copy-done.15), channel_id=1, source_target_pairs={{0,2},{1,3},{2,0},{3,1},{4,6},{5,7},{6,4},{7,5},{8,10},{9,11},{10,... | collective-permute-start | bytes 1179656 | tf_op jit(solution)/shard_map/ppermute | solution.py:492
  109.0 2.7 %all-to-all-done.1 = bf16[32,8,384]{2,1,0:T(8,128)(2,1)S(1)} async-done(((bf16[32,8,384]{2,1,0:T(8,128)(2,1)}), bf16[32,8,384]{2,1,0:T(8,128)(2,1)S(1)}, u32[]{:S(2)}, u32[]{:S(2)}) %all-to-all-start.1) | async-done | bytes 196640 | tf_op jit(solution)/shard_map/all_to_all | solution.py:499
  113.1 16.8 %collective-permute-done.10 = bf16[2048,96]{1,0:T(8,128)(2,1)S(1)} collective-permute-done((bf16[2048,96]{1,0:T(8,128)(2,1)}, bf16[2048,96]{1,0:T(8,128)(2,1)S(1)}, u32[]{:S(2)}, u32[]{:S(2)}) %collective-permute-start.10) | collective-permute-done | bytes 393248 | tf_op jit(solution)/shard_map/ppermute | solution.py:492
  129.9 3.3 %collective-permute-done.8 = bf16[2048,96]{1,0:T(8,128)(2,1)S(1)} collective-permute-done((bf16[2048,96]{1,0:T(8,128)(2,1)}, bf16[2048,96]{1,0:T(8,128)(2,1)S(1)}, u32[]{:S(2)}, u32[]{:S(2)}) %collective-permute-start.8) | collective-permute-done | bytes 393248 | tf_op jit(solution)/shard_map/ppermute | solution.py:492
  (53 shorter events, 17.0 us)
Async XLA Ops:
  1.4 1.4 %copy-start = (bf16[8,16,16,384]{3,2,1,0:T(8,128)(2,1)S(1)}, bf16[8,16,16,384]{3,2,1,0:T(8,128)(2,1)}, u32[]{:S(2)}) copy-start(bf16[8,16,16,384]{3,2,1,0:T(8,128)(2,1)} %param.5) | copy-start | bytes 4718596
  2.8 1.4 %copy-start.2 = (bf16[8,16,16,384]{3,2,1,0:T(8,128)(2,1)S(1)}, bf16[8,16,16,384]{3,2,1,0:T(8,128)(2,1)}, u32[]{:S(2)}) copy-start(bf16[8,16,16,384]{3,2,1,0:T(8,128)(2,1)} %param.9) | copy-start | bytes 4718596
  7.2 2.6 %collective-permute-start = (bf16[25,16,128]{2,1,0:T(8,128)(2,1)S(1)}, bf16[25,16,128]{2,1,0:T(8,128)(2,1)S(1)}, u32[]{:S(2)}, u32[]{:S(2)}) collective-permute-start(bf16[25,16,128]{2,1,0:T(8,128)(2,1)S(1)} %get-tuple-element.32), channel_id=1, source_target_pairs={{0,4},{4,8},{8,12},{1,5},{5,9},{9,13},{2,6},{6,10},{10,14},{3,7},{... | collective-permute-start | bytes 307208 | tf_op jit(solution)/shard_map/ppermute | solution.py:372
  8.5 6.6 %collective-permute-start.1 = (bf16[25,16,128]{2,1,0:T(8,128)(2,1)S(1)}, bf16[25,16,128]{2,1,0:T(8,128)(2,1)S(1)}, u32[]{:S(2)}, u32[]{:S(2)}) collective-permute-start(bf16[25,16,128]{2,1,0:T(8,128)(2,1)S(1)} %get-tuple-element.33), channel_id=1, source_target_pairs={{4,0},{8,4},{12,8},{5,1},{9,5},{13,9},{6,2},{10,6},{14,10},{7,3},{... | collective-permute-start | bytes 307208 | tf_op jit(solution)/shard_map/ppermute | solution.py:373
  15.1 9.5 %collective-permute-start.2 = (bf16[69,16,128]{2,1,0:T(8,128)(2,1)S(1)}, bf16[69,16,128]{2,1,0:T(8,128)(2,1)S(1)}, u32[]{:S(2)}, u32[]{:S(2)}) collective-permute-start(bf16[69,16,128]{2,1,0:T(8,128)(2,1)S(1)} %get-tuple-element.41), channel_id=1, source_target_pairs={{0,16},{16,32},{32,48},{48,64},{64,80},{80,96},{96,112},{1,17},{17... | collective-permute-start | bytes 847880 | tf_op jit(solution)/shard_map/ppermute | solution.py:372
  17.7 11.9 %collective-permute-start.3 = (bf16[69,16,128]{2,1,0:T(8,128)(2,1)S(1)}, bf16[69,16,128]{2,1,0:T(8,128)(2,1)S(1)}, u32[]{:S(2)}, u32[]{:S(2)}) collective-permute-start(bf16[69,16,128]{2,1,0:T(8,128)(2,1)S(1)} %get-tuple-element.42), channel_id=1, source_target_pairs={{16,0},{32,16},{48,32},{64,48},{80,64},{96,80},{112,96},{17,1},{33... | collective-permute-start | bytes 847880 | tf_op jit(solution)/shard_map/ppermute | solution.py:373
  41.0 18.3 %collective-permute-start.4 = (bf16[66,16,128]{2,1,0:T(8,128)(2,1)S(1)}, bf16[66,16,128]{2,1,0:T(8,128)(2,1)S(1)}, u32[]{:S(2)}, u32[]{:S(2)}) collective-permute-start(bf16[66,16,128]{2,1,0:T(8,128)(2,1)S(1)} %get-tuple-element.48), channel_id=1, source_target_pairs={{0,16},{16,32},{32,48},{48,64},{64,80},{80,96},{96,112},{1,17},{17... | collective-permute-start | bytes 811016 | tf_op jit(solution)/shard_map/ppermute | solution.py:372
  46.2 13.2 %collective-permute-start.5 = (bf16[66,16,128]{2,1,0:T(8,128)(2,1)S(1)}, bf16[66,16,128]{2,1,0:T(8,128)(2,1)S(1)}, u32[]{:S(2)}, u32[]{:S(2)}) collective-permute-start(bf16[66,16,128]{2,1,0:T(8,128)(2,1)S(1)} %get-tuple-element.49), channel_id=1, source_target_pairs={{16,0},{32,16},{48,32},{64,48},{80,64},{96,80},{112,96},{17,1},{33... | collective-permute-start | bytes 811016 | tf_op jit(solution)/shard_map/ppermute | solution.py:373
  47.5 21.7 %copy-start.3 = (bf16[8,16,16,384]{3,2,1,0:T(8,128)(2,1)S(1)}, bf16[8,16,16,384]{3,2,1,0:T(8,128)(2,1)}, u32[]{:S(2)}) copy-start(bf16[8,16,16,384]{3,2,1,0:T(8,128)(2,1)} %param.9) | copy-start | bytes 4718596
  59.3 2.0 %copy-start.12 = (bf16[8,16,16,128]{3,2,1,0:T(8,128)(2,1)}, bf16[8,16,16,128]{3,2,1,0:T(8,128)(2,1)S(1)}, u32[]{:S(2)}) copy-start(bf16[8,16,16,128]{3,2,1,0:T(8,128)(2,1)S(1)} %get-tuple-element.46.qa) | copy-start | bytes 1572868
  59.3 9.9 %copy-start.1 = (bf16[8,16,16,384]{3,2,1,0:T(8,128)(2,1)S(1)}, bf16[8,16,16,384]{3,2,1,0:T(8,128)(2,1)}, u32[]{:S(2)}) copy-start(bf16[8,16,16,384]{3,2,1,0:T(8,128)(2,1)} %param.5) | copy-start | bytes 4718596
  60.1 1.1 copy-start.4
  61.3 7.4 %collective-permute-start.6 = (bf16[24,16,128]{2,1,0:T(8,128)(2,1)}, bf16[24,16,128]{2,1,0:T(8,128)(2,1)S(1)}, u32[]{:S(2)}, u32[]{:S(2)}) collective-permute-start(bf16[24,16,128]{2,1,0:T(8,128)(2,1)} %get-tuple-element.50), channel_id=1, source_target_pairs={{0,4},{4,8},{8,12},{1,5},{5,9},{9,13},{2,6},{6,10},{10,14},{3,7},{... | collective-permute-start | bytes 294920 | tf_op jit(solution)/shard_map/ppermute | solution.py:372
  65.7 3.5 %collective-permute-start.7 = (bf16[24,16,128]{2,1,0:T(8,128)(2,1)}, bf16[24,16,128]{2,1,0:T(8,128)(2,1)}, u32[]{:S(2)}, u32[]{:S(2)}) collective-permute-start(bf16[24,16,128]{2,1,0:T(8,128)(2,1)} %get-tuple-element.51), channel_id=1, source_target_pairs={{4,0},{8,4},{12,8},{5,1},{9,5},{13,9},{6,2},{10,6},{14,10},{7,3},{... | collective-permute-start | bytes 294920 | tf_op jit(solution)/shard_map/ppermute | solution.py:373
  69.2 1.4 %copy-start.5 = (f32[8,22,16,128]{3,2,1,0:T(8,128)S(1)}, f32[8,22,16,128]{3,2,1,0:T(8,128)}, u32[]{:S(2)}) copy-start(f32[8,22,16,128]{3,2,1,0:T(8,128)} %copy-done.4) | copy-start | bytes 4325380
  70.6 1.0 copy-start.7
  71.5 0.9 copy-start.10
  72.4 1.0 copy-start.13
  76.4 1.0 copy-start.8
  79.7 53.5 %copy-start.9 = (f32[2048,96]{1,0:T(8,128)S(1)}, f32[2048,96]{1,0:T(8,128)}, u32[]{:S(2)}) copy-start(f32[2048,96]{1,0:T(8,128)} %copy-done.8) | copy-start | bytes 2359300
  99.4 12.3 %all-to-all-start.1 = ((bf16[32,8,384]{2,1,0:T(8,128)(2,1)}), bf16[32,8,384]{2,1,0:T(8,128)(2,1)S(1)}, u32[]{:S(2)}, u32[]{:S(2)}) async-start(bf16[32,8,384]{2,1,0:T(8,128)(2,1)} %broadcast_in_dim.2), calls=%async_computation.1 | async-start | bytes 393216 | tf_op jit(solution)/shard_map/all_to_all | solution.py:499
  103.7 26.3 %collective-permute-start.10 = (bf16[2048,96]{1,0:T(8,128)(2,1)}, bf16[2048,96]{1,0:T(8,128)(2,1)S(1)}, u32[]{:S(2)}, u32[]{:S(2)}) collective-permute-start(bf16[2048,96]{1,0:T(8,128)(2,1)} %copy-done.17), channel_id=1, source_target_pairs={{0,3},{1,0},{2,1},{3,2},{4,7},{5,4},{6,5},{7,6},{8,11},{9,8},{10,9... | collective-permute-start | bytes 1179656 | tf_op jit(solution)/shard_map/ppermute | solution.py:492
  106.7 26.5 %collective-permute-start.8 = (bf16[2048,96]{1,0:T(8,128)(2,1)}, bf16[2048,96]{1,0:T(8,128)(2,1)S(1)}, u32[]{:S(2)}, u32[]{:S(2)}) collective-permute-start(bf16[2048,96]{1,0:T(8,128)(2,1)} %copy-done.16), channel_id=1, source_target_pairs={{0,1},{1,2},{2,3},{3,0},{4,5},{5,6},{6,7},{7,4},{8,9},{9,10},{10,1... | collective-permute-start | bytes 1179656 | tf_op jit(solution)/shard_map/ppermute | solution.py:492
  106.8 26.5 %collective-permute-start.9 = (bf16[2048,96]{1,0:T(8,128)(2,1)}, bf16[2048,96]{1,0:T(8,128)(2,1)S(1)}, u32[]{:S(2)}, u32[]{:S(2)}) collective-permute-start(bf16[2048,96]{1,0:T(8,128)(2,1)} %copy-done.15), channel_id=1, source_target_pairs={{0,2},{1,3},{2,0},{3,1},{4,6},{5,7},{6,4},{7,5},{8,10},{9,11},{10,... | collective-permute-start | bytes 1179656 | tf_op jit(solution)/shard_map/ppermute | solution.py:492
  (6 other events, 4.8 us)
